TPU v7x, 128 devices: a whole 4x4x4 slice. The times are simulated.
128 devices in a mesh: user: 16 (over y, z), item: 8 (over x, core).
Axes of the slice: x: 4, y: 4, z: 4, core: 2. Of those that a mesh axis runs over, the one named last changes fastest.
Arguments:
- tile_values: bfloat16 [256, 32, 256, 128], P('user', 'item'), may hold values from -600 to 600
- tile_ids: int32 [256, 32], P('user', 'item'), may hold values from 0 to 2047, as said below
- lengths: int32 [256], P('user'), may hold values from 128 to 256
- user_weights: float32 [256, 256], P('user'), may hold values from 0.5 to 16
- time_factor: float32 [256, 256], replicated, may hold values from -0.25 to 2.25
- item_factor: bfloat16 [262144, 256], P(('item', 'user')), may hold values from -0.2421875 to 0.2421875
Outputs:
- slices: bfloat16 [256, 256, 256], P(('user', 'item'))
- new_time: float32 [256, 256], replicated
- new_items: float32 [262144, 256], P(('item', 'user'))
Inputs may be any that keep to these rules, and one draw needn't show every extreme that they name: `tile_ids`: slot block i of a user (slots i * 4 to (i + 1) * 4 - 1) names tiles i * 256 to (i + 1) * 256 - 1. Within the slots of 16 users of one index of user in one slot block, all tiles differ, and at most 8 of them lie in one group of 16 tiles (group g: tiles i * 256 + g * 16 onward); in every slot block some group holds exactly 8 of them for every index of user.
All inputs are finite; a program needn't handle non-finite values.
Results may differ from a plain program's by a relative error of at most 0.014.
Values may be sent and summed in bfloat16 or wider, within the bound.
A program may use at most 128 MiB of HBM per device.

v0:
```python
import jax
import jax.numpy as jnp
from jax import lax
from jax.sharding import PartitionSpec as P

NS_STEPS = 6


HIGHEST_PRECISION = lax.Precision.HIGHEST
EPSILON = 1e-06


def polar_batch(target):
    norm_scale = jnp.sqrt(jnp.sum(target * target, axis=(1, 2), keepdims=True) + EPSILON)
    iterate = target / norm_scale
    for sweep_index in range(NS_STEPS):
        inner_gram = jnp.einsum("krc,krd->kcd", iterate, iterate, precision=HIGHEST_PRECISION)
        iterate = 1.5 * iterate - 0.5 * jnp.einsum(
            "krc,kcd->krd", iterate, inner_gram, precision=HIGHEST_PRECISION
        )
    return iterate


def spd_solve(gram_matrix, right_side):
    chol_lower = jnp.linalg.cholesky(gram_matrix)
    return jax.scipy.linalg.cho_solve((chol_lower, True), right_side.T).T


def body(tile_values, tile_ids, lengths, user_weights, time_factor, item_factor):
    user_count = lax.axis_size("user")
    item_count = lax.axis_size("item")
    item_pos = lax.axis_index("item")
    users_here, slots_user, time_rows, tile_width = tile_values.shape
    rank_size = time_factor.shape[0]
    tiles_owned = item_factor.shape[0] // tile_width
    slot_count = users_here * slots_user
    share_count = users_here // item_count
    local_ids = tile_ids - item_pos * (tiles_owned * user_count)
    flat_ids = local_ids.reshape(slot_count)
    live_rows = (jnp.arange(time_rows, dtype=jnp.int32)[None, :] < lengths[:, None]).astype(
        tile_values.dtype
    )
    masked = tile_values * live_rows[:, None, :, None]
    shard_rows = lax.all_gather(item_factor, "user", axis=0, tiled=True)
    panels = shard_rows.reshape(tiles_owned * user_count, tile_width, rank_size)[flat_ids]
    panels = panels.reshape(users_here, slots_user, tile_width, rank_size)
    partial_value = jnp.einsum("ksrt,kstc->krc", masked, panels, preferred_element_type=jnp.float32)
    share_start = item_pos * share_count
    share_weights = lax.dynamic_slice_in_dim(user_weights, share_start, share_count, 0)
    projection = lax.psum(partial_value, "item")
    scaled_all = projection * user_weights[:, None, :]
    polar_all = polar_batch(
        jnp.einsum("krc,dc->krd", scaled_all, time_factor, precision=HIGHEST_PRECISION)
    )
    polar_share = lax.dynamic_slice_in_dim(polar_all, share_start, share_count, 0)
    scaled = lax.dynamic_slice_in_dim(scaled_all, share_start, share_count, 0)
    time_term = jnp.einsum("krc,krd->cd", polar_share, scaled, precision=HIGHEST_PRECISION)
    weight_term = jnp.dot(
        share_weights.T,
        share_weights,
        precision=HIGHEST_PRECISION,
        preferred_element_type=jnp.float32,
    )
    item_term = jnp.dot(item_factor.T, item_factor, preferred_element_type=jnp.float32)
    time_mttkrp, weight_gram, item_inner = lax.psum(
        (time_term, weight_term, item_term), ("user", "item")
    )
    time_raw = spd_solve(item_inner * weight_gram, time_mttkrp)
    new_time = time_raw / jnp.sqrt(jnp.sum(time_raw * time_raw, axis=0, keepdims=True) + EPSILON)
    item_gram = (
        jnp.dot(
            new_time.T, new_time, precision=HIGHEST_PRECISION, preferred_element_type=jnp.float32
        )
        * weight_gram
    )
    user_maps = (
        jnp.einsum("krc,cd->krd", polar_all, new_time, precision=HIGHEST_PRECISION)
        * user_weights[:, None, :]
    ).astype(jnp.bfloat16)
    tile_terms = jnp.einsum(
        "ksrt,krc->kstc", masked, user_maps, preferred_element_type=jnp.float32
    ).astype(jnp.bfloat16)
    tile_terms = tile_terms.reshape(slot_count, tile_width * rank_size)
    row_count = tiles_owned * tile_width * lax.axis_size("user")
    wanted_tiles = jnp.arange(row_count // tile_width, dtype=jnp.int32)
    hit_table = (flat_ids[None, :] == wanted_tiles[:, None]).astype(jnp.bfloat16)
    summed = jnp.dot(hit_table, tile_terms, preferred_element_type=jnp.float32)
    item_mttkrp = lax.psum_scatter(
        summed.reshape(row_count, rank_size).astype(jnp.bfloat16),
        "user",
        scatter_dimension=0,
        tiled=True,
    ).astype(jnp.float32)
    new_items = spd_solve(item_gram, item_mttkrp)
    return (polar_share.astype(jnp.bfloat16), new_time, new_items)


def solution(mesh):
    in_specs = (
        P("user", "item", None, None),
        P("user", "item"),
        P("user"),
        P("user", None),
        P(),
        P(("item", "user"), None),
    )
    out_specs = (P(("user", "item"), None, None), P(), P(("item", "user"), None))
    return jax.shard_map(body, mesh=mesh, in_specs=in_specs, out_specs=out_specs, check_vma=False)
```

profile of v0, /device:TPU:1, one launch (start us, length us, event | category | flops | bytes accessed | tf_op | source)
XLA Modules:
  0.0 677.0 jit_solution(8899819774510441015)
XLA Ops:
  9.6 114.9 %all-gather.2.cloned.1.call-done = bf16[32768,256]{1,0:T(8,128)(2,1)} async-done(((bf16[2048,256]{1,0:T(8,128)(2,1)}), bf16[32768,256]{1,0:T(8,128)(2,1)}) %all-gather.2.cloned.1.call-update) | async-done | bytes 16777232 | tf_op jit(solution)/shard_map/all_gather | solution.py:44
  124.5 8.5 %gather_fusion = bf16[64,128,256]{2,1,0:T(8,128)(2,1)} fusion(bf16[256,128,256]{2,1,0:T(8,128)(2,1)} %bitcast.132, s32[1024]{0:T(1024)S(1)} %pad_clamp_fusion), kind=kCustom, calls=%fused_computation | custom fusion | bytes 8388864 | tf_op jit(solution)/shard_map/gather | solution.py:45
  133.0 6.7 fusion.7
  142.8 67.4 %all-reduce.5.cloned.1.call-done = f32[16,256,256]{2,1,0:T(8,128)} async-done(((f32[16,256,256]{2,1,0:T(8,128)}), f32[16,256,256]{2,1,0:T(8,128)}) %all-reduce.5.cloned.1.call-update) | async-done | bytes 4194320 | tf_op jit(solution)/shard_map/psum | solution.py:50
  212.8 3.6 multiply_reduce_fusion
  216.4 7.5 %fusion.13 = f32[16,256,256]{2,1,0:T(8,128)S(1)} fusion(f32[16,256,256]{2,1,0:T(8,128)S(1)} %get-tuple-element.58, f32[16]{0:T(128)S(1)} %add_sqrt_fusion.1), kind=kOutput, calls=%fused_computation.34 | convolution fusion | flops 3222274048 | bytes 8388672 | tf_op jit(solution)/shard_map/krc,krd->kcd/dot_general | solution.py:17
  223.9 4.9 multiply_subtract_fusion.5
  228.8 7.0 %fusion.54 = f32[16,256,256]{2,1,0:T(8,128)S(1)} fusion(f32[16,256,256]{2,1,0:T(8,128)S(1)} %multiply_subtract_fusion.5), kind=kOutput, calls=%fused_computation.109 | convolution fusion | flops 3221225472 | bytes 8388608 | tf_op jit(solution)/shard_map/krc,krd->kcd/dot_general | solution.py:17
  235.8 4.9 multiply_subtract_fusion.4
  240.6 7.0 %fusion.55 = f32[16,256,256]{2,1,0:T(8,128)S(1)} fusion(f32[16,256,256]{2,1,0:T(8,128)S(1)} %multiply_subtract_fusion.4), kind=kOutput, calls=%fused_computation.110 | convolution fusion | flops 3221225472 | bytes 8388608 | tf_op jit(solution)/shard_map/krc,krd->kcd/dot_general | solution.py:17
  247.6 4.9 multiply_subtract_fusion.3
  252.5 7.2 %fusion.56 = f32[16,256,256]{2,1,0:T(8,128)S(1)} fusion(f32[16,256,256]{2,1,0:T(8,128)S(1)} %multiply_subtract_fusion.3), kind=kOutput, calls=%fused_computation.111 | convolution fusion | flops 3221225472 | bytes 8388608 | tf_op jit(solution)/shard_map/krc,krd->kcd/dot_general | solution.py:17
  259.7 4.9 multiply_subtract_fusion.2
  264.6 7.0 %fusion.57 = f32[16,256,256]{2,1,0:T(8,128)S(1)} fusion(f32[16,256,256]{2,1,0:T(8,128)S(1)} %multiply_subtract_fusion.2), kind=kOutput, calls=%fused_computation.112 | convolution fusion | flops 3221225472 | bytes 8388608 | tf_op jit(solution)/shard_map/krc,krd->kcd/dot_general | solution.py:17
  271.5 4.9 multiply_subtract_fusion.1
  276.4 7.2 %fusion.58 = f32[16,256,256]{2,1,0:T(8,128)S(1)} fusion(f32[16,256,256]{2,1,0:T(8,128)S(1)} %multiply_subtract_fusion.1), kind=kOutput, calls=%fused_computation.113 | convolution fusion | flops 3221225472 | bytes 8388608 | tf_op jit(solution)/shard_map/krc,krd->kcd/dot_general | solution.py:17
  283.6 4.9 multiply_subtract_fusion
  292.4 150.0 %all-reduce.7.cloned.1.call-done = (f32[256,256]{1,0:T(8,128)}, f32[256,256]{0,1:T(8,128)}, f32[256,256]{0,1:T(8,128)}) async-done(((f32[256,256]{1,0:T(8,128)}, f32[256,256]{0,1:T(8,128)}, f32[256,256]{0,1:T(8,128)}), (f32[256,256]{1,0:T(8,128)}, f32[256,256]{0,1:T(8,128)}, f32[256,256]{0,1:T(8,128)})) %all-reduce.7.cloned.1.call-update) | async-done | bytes 786448 | tf_op jit(solution)/shard_map/psum | solution.py:65
  443.7 11.7 %cholesky.130 = f32[128,128]{1,0:T(8,128)S(1)} custom-call(f32[128,128]{1,0:T(8,128)S(1)} %cholesky.194), custom_call_target="Cholesky" | custom-call | tf_op jit(solution)/shard_map/jit(cholesky)/cholesky | solution.py:25
  455.4 9.8 %custom-call.25 = f32[1,128,128]{1,2,0:T(8,128)S(1)} custom-call(f32[1,128,128]{2,1,0:T(8,128)S(1)} %get-tuple-element.56), custom_call_target="InvertDiagBlocksLowerTriangular" | custom-call | tf_op jit(solution)/shard_map/jit(cholesky)/cholesky | solution.py:25
  465.7 11.7 %cholesky.147 = f32[128,128]{1,0:T(8,128)S(1)} custom-call(f32[128,128]{1,0:T(8,128)S(1)} %convolution_subtract_fusion.5), custom_call_target="Cholesky" | custom-call | tf_op jit(solution)/shard_map/jit(cholesky)/cholesky | solution.py:25
  479.6 4.2 while.2
  483.7 19.7 %custom-call.22 = f32[2,128,128]{1,2,0:T(8,128)S(1)} custom-call(f32[2,128,128]{2,1,0:T(8,128)S(1)} %get-tuple-element.11), custom_call_target="InvertDiagBlocksLowerTriangular" | custom-call | tf_op jit(solution)/shard_map/jit(_cho_solve)/triangular_solve | solution.py:26
  505.3 5.7 multiply_convert_fusion
  516.1 8.1 %convolution_convert_fusion = bf16[256,32768]{1,0:T(8,128)(2,1)} fusion(bf16[64,32768]{1,0:T(8,128)(2,1)S(1)} %bitcast.131, s32[64]{0:T(128)S(1)} %eq.15), kind=kOutput, calls=%fused_computation.5 | convolution fusion | flops 1082146816 | bytes 20971776 | tf_op jit(solution)/shard_map/dot_general | solution.py:87
  524.1 25.8 %convert_element_type.29 = bf16[32768,256]{1,0:T(8,128)(2,1)} reshape(bf16[256,32768]{1,0:T(8,128)(2,1)} %convolution_convert_fusion) | data formatting | bytes 33554432 | tf_op jit(solution)/shard_map/convert_element_type | solution.py:89
  553.4 11.7 %cholesky.164 = f32[128,128]{1,0:T(8,128)S(1)} custom-call(f32[128,128]{1,0:T(8,128)S(1)} %cholesky.197), custom_call_target="Cholesky" | custom-call | tf_op jit(solution)/shard_map/jit(cholesky)/cholesky | solution.py:25
  565.2 9.8 %custom-call.26 = f32[1,128,128]{1,2,0:T(8,128)S(1)} custom-call(f32[1,128,128]{2,1,0:T(8,128)S(1)} %get-tuple-element.52), custom_call_target="InvertDiagBlocksLowerTriangular" | custom-call | tf_op jit(solution)/shard_map/jit(cholesky)/cholesky | solution.py:25
  575.5 11.7 %cholesky.181 = f32[128,128]{1,0:T(8,128)S(1)} custom-call(f32[128,128]{1,0:T(8,128)S(1)} %convolution_subtract_fusion.4), custom_call_target="Cholesky" | custom-call | tf_op jit(solution)/shard_map/jit(cholesky)/cholesky | solution.py:25
  589.8 3.8 while.3
  593.6 19.9 %custom-call.23 = f32[2,128,128]{1,2,0:T(8,128)S(1)} custom-call(f32[2,128,128]{2,1,0:T(8,128)S(1)} %get-tuple-element.19), custom_call_target="InvertDiagBlocksLowerTriangular" | custom-call | tf_op jit(solution)/shard_map/jit(_cho_solve)/triangular_solve | solution.py:26
  613.6 45.8 %reduce-scatter.2.cloned.1.call-done = bf16[2048,256]{1,0:T(8,128)(2,1)} async-done(((bf16[32768,256]{1,0:T(8,128)(2,1)}), bf16[2048,256]{1,0:T(8,128)(2,1)}) %reduce-scatter.2.cloned.1.call-update) | async-done | bytes 1048592 | tf_op jit(solution)/shard_map/reduce_scatter | solution.py:88
  (96 shorter events, 45.0 us)
Async XLA Ops:
  7.2 205.6 %copy-start = (f32[256,256]{1,0:T(8,128)S(1)}, f32[256,256]{1,0:T(8,128)}, u32[]{:S(2)}) copy-start(f32[256,256]{1,0:T(8,128)} %param.11) | copy-start | bytes 786436
  7.2 117.4 %all-gather.2.cloned.1.call-start = ((), (), s32[]{:S(2)}) async-start(), calls=%async_computation.1 | async-start | bytes 17825792 | tf_op jit(solution)/shard_map/all_gather | solution.py:44
  7.9 202.3 %all-reduce.5.cloned.1.call-start = ((), (), s32[]{:S(2)}) async-start(), calls=%async_computation.2 | async-start | bytes 8388608 | tf_op jit(solution)/shard_map/psum | solution.py:50
  139.7 0.7 copy-start.7
  139.7 1.9 copy-start.4
  139.8 302.6 %all-reduce.7.cloned.1.call-start = ((), (), s32[]{:S(2)}) async-start(), calls=%async_computation.4 | async-start | bytes 1572864 | tf_op jit(solution)/shard_map/psum | solution.py:65
  288.4 2.0 copy-start.2
  292.2 367.1 %reduce-scatter.2.cloned.1.call-start = ((), (), s32[]{:S(2)}) async-start(), calls=%async_computation.3 | async-start | bytes 17825792 | tf_op jit(solution)/shard_map/reduce_scatter | solution.py:88
  442.4 61.1 %copy-start.6 = (f32[256,256]{1,0:T(8,128)S(1)}, f32[256,256]{1,0:T(8,128)}, u32[]{:S(2)}) copy-start(f32[256,256]{1,0:T(8,128)} %get-tuple-element.42) | copy-start | bytes 786436
  504.0 7.1 %copy-start.3 = (bf16[16,4,256,128]{3,2,1,0:T(8,128)(2,1)S(1)}, bf16[16,4,256,128]{3,2,1,0:T(8,128)(2,1)}, u32[]{:S(2)}) copy-start(bf16[16,4,256,128]{3,2,1,0:T(8,128)(2,1)} %param.7) | copy-start | bytes 12582916
  549.9 2.8 copy-start.5
  667.0 3.0 copy-start.1
Sparse Core Ops, SparseCore 0:
  10.1 114.3 all-gather.1
  139.9 70.2 all-reduce.4
  292.3 149.9 all-reduce.6
  550.1 109.2 reduce-scatter.1
where the time goes:
time: 688 us; the launch traced here: 677 us
  waiting for transfers between devices  379 us (55%)
  other arithmetic  114 us (17%)
  matrix products  114 us (17%)
  local copies, waits for them, and re-layouts  52.5 us (8%)
  between operations  17.2 us (2%)
    psum x1, waiting for transfers between devices, body(): lax.psum((time_term, weight_term, item_term), ('user', 'item'))  150 us
    all_gather x1, waiting for transfers between devices, body(): shard_rows = lax.all_gather(item_factor, 'user', axis=0, tiled=True)  115 us
    another operation x13, other arithmetic, spd_solve(): chol_lower = jnp.linalg.cholesky(gram_matrix)  68.5 us
    psum x1, waiting for transfers between devices, body(): projection = lax.psum(partial_value, 'item')  67.4 us
    reduce_scatter x1, waiting for transfers between devices, body(): lax.psum_scatter(summed.reshape(row_count, rank_size).astype(jnp.bfloat16...  45.8 us
    dot_general x6, matrix products, polar_batch(): jnp.einsum('krc,krd->kcd', iterate, iterate, precision=HIGHEST_PRECISION)  42.8 us
    another operation x5, other arithmetic, spd_solve(): return jax.scipy.linalg.cho_solve((chol_lower, True), right_side.T).T  39.7 us
    dot_general x6, matrix products, polar_batch(): jnp.einsum('krc,kcd->krd', iterate, inner_gram, precision=HIGHEST_PRECISION)  29.2 us
  transfers between devices with their start and end apart: 4, of which 4 were waited for; matrix products, arithmetic and copies ran while one was open for 10% of the time, Pallas kernels for 0%

commit v1 on v0

v1 whole, which is shorter than its diff:
```python
import jax
import jax.numpy as jnp
from jax import lax
from jax.sharding import PartitionSpec as P

NS_STEPS = 6
HIGHEST = lax.Precision.HIGHEST
EPSILON = 1e-06


def polar_batch(target):
    norm_scale = jnp.sqrt(jnp.sum(target * target, axis=(1, 2), keepdims=True) + EPSILON)
    iterate = target / norm_scale
    for _ in range(NS_STEPS):
        gram = jnp.einsum("krc,krd->kcd", iterate, iterate, precision=HIGHEST)
        iterate = 1.5 * iterate - 0.5 * jnp.einsum("krc,kcd->krd", iterate, gram, precision=HIGHEST)
    return iterate


def spd_solve(gram_matrix, right_side):
    chol_lower = jnp.linalg.cholesky(gram_matrix)
    return jax.scipy.linalg.cho_solve((chol_lower, True), right_side.T).T


def body(tile_values, tile_ids, lengths, user_weights, time_factor, item_factor):
    user_count = lax.axis_size("user")
    item_count = lax.axis_size("item")
    item_pos = lax.axis_index("item")
    users_here, slots_user, time_rows, tile_width = tile_values.shape
    rank_size = time_factor.shape[0]
    tiles_owned = item_factor.shape[0] // tile_width
    slot_count = users_here * slots_user
    share_count = users_here // item_count
    flat_ids = (tile_ids - item_pos * (tiles_owned * user_count)).reshape(slot_count)
    live = jnp.arange(time_rows, dtype=jnp.int32)[None, :] < lengths[:, None]
    shard_rows = lax.all_gather(item_factor, "user", axis=0, tiled=True)
    panels = shard_rows.reshape(tiles_owned * user_count, tile_width, rank_size)[flat_ids]
    panels = panels.reshape(users_here, slots_user, tile_width, rank_size)
    partial = jnp.einsum("ksrt,kstc->krc", tile_values, panels, preferred_element_type=jnp.float32)
    partial = jnp.where(live[:, :, None], partial, 0.0)
    share_start = item_pos * share_count
    share_weights = lax.dynamic_slice_in_dim(user_weights, share_start, share_count, 0)
    projection = lax.psum_scatter(partial, "item", scatter_dimension=0, tiled=True)
    scaled = projection * share_weights[:, None, :]
    polar = polar_batch(jnp.einsum("krc,dc->krd", scaled, time_factor, precision=HIGHEST))
    slices = polar.astype(jnp.bfloat16)
    time_term = jnp.einsum("krc,krd->cd", polar, scaled, precision=HIGHEST)
    weight_term = jnp.dot(share_weights.T, share_weights, precision=HIGHEST)
    item_term = jnp.dot(item_factor.T, item_factor, preferred_element_type=jnp.float32)
    sums = lax.psum((time_term, weight_term, item_term), "item")
    time_mttkrp, weight_gram, item_inner = lax.psum(sums, "user")
    polar_all = lax.all_gather(slices, "item", axis=0, tiled=True).astype(jnp.float32)
    time_raw = spd_solve(item_inner * weight_gram, time_mttkrp)
    new_time = time_raw / jnp.sqrt(jnp.sum(time_raw * time_raw, axis=0, keepdims=True) + EPSILON)
    item_gram = jnp.dot(new_time.T, new_time, precision=HIGHEST) * weight_gram
    user_maps = (
        jnp.einsum("krc,cd->krd", polar_all, new_time, precision=HIGHEST) * user_weights[:, None, :]
    )
    user_maps = jnp.where(live[:, :, None], user_maps, 0.0).astype(jnp.bfloat16)
    tile_terms = jnp.einsum(
        "ksrt,krc->kstc", tile_values, user_maps, preferred_element_type=jnp.float32
    ).astype(jnp.bfloat16)
    tile_terms = tile_terms.reshape(slot_count, tile_width * rank_size)
    row_count = tiles_owned * tile_width * user_count
    wanted = jnp.arange(row_count // tile_width, dtype=jnp.int32)
    hits = (flat_ids[None, :] == wanted[:, None]).astype(jnp.bfloat16)
    summed = jnp.dot(hits, tile_terms, preferred_element_type=jnp.float32)
    item_mttkrp = lax.psum_scatter(
        summed.reshape(row_count, rank_size).astype(jnp.bfloat16),
        "user",
        scatter_dimension=0,
        tiled=True,
    ).astype(jnp.float32)
    new_items = spd_solve(item_gram, item_mttkrp)
    return (slices, new_time, new_items)


def solution(mesh):
    in_specs = (
        P("user", "item", None, None),
        P("user", "item"),
        P("user"),
        P("user", None),
        P(),
        P(("item", "user"), None),
    )
    out_specs = (P(("user", "item"), None, None), P(), P(("item", "user"), None))
    return jax.shard_map(body, mesh=mesh, in_specs=in_specs, out_specs=out_specs, check_vma=False)
```

time: 688 us -> 618 us (0.90)
  matrix products: 114 us -> 53 us
  waiting for transfers between devices: 379 us -> 349 us
  local copies, waits for them, and re-layouts: 52.5 us -> 74.3 us
    psum x2, waiting for transfers between devices: 217 us -> 152 us  [the longest x1 89.9 us: body(): time_mttkrp, weight_gram, item_inner = lax.psum(sums, 'user')]
    dot_general x20, matrix products: 102 us -> 41.2 us  [the longest x1 10.2 us: body(): summed = jnp.dot(hits, tile_terms, preferred_element_type=jnp.float32)]
    reduce_scatter x0 -> x1, waiting for transfers between devices: none -> 31.8 us  [body(): lax.psum_scatter(partial, 'item', scatter_dimension=0, tiled=True)]
    convert_element_type x1 -> x2, local copies, waits for them, and re-layouts: 25.8 us -> 47.1 us  [body(): summed.reshape(row_count, rank_size).astype(jnp.bfloat16)]
  transfers between devices with their start and end apart: 4 -> 6, of which waited for: 4 -> 5; matrix products, arithmetic and copies ran while one was open for 10% -> 21% of each run, Pallas kernels for 0% -> 0%
where the time goes in v1:
time: 618 us; the launch traced here: 606 us
  waiting for transfers between devices  349 us (56%)
  other arithmetic  111 us (18%)
  local copies, waits for them, and re-layouts  74.3 us (12%)
  matrix products  53 us (9%)
  between operations  17.7 us (3%)
    all_gather x1, waiting for transfers between devices, body(): shard_rows = lax.all_gather(item_factor, 'user', axis=0, tiled=True)  115 us
    psum x1, waiting for transfers between devices, body(): time_mttkrp, weight_gram, item_inner = lax.psum(sums, 'user')  89.9 us
    another operation x13, other arithmetic, spd_solve(): chol_lower = jnp.linalg.cholesky(gram_matrix)  68.7 us
    psum x1, waiting for transfers between devices, body(): sums = lax.psum((time_term, weight_term, item_term), 'item')  61.9 us
    reduce_scatter x1, waiting for transfers between devices, body(): lax.psum_scatter(summed.reshape(row_count, rank_size).astype(jnp.bfloat16...  49.7 us
    convert_element_type x2, local copies, waits for them, and re-layouts, body(): summed.reshape(row_count, rank_size).astype(jnp.bfloat16)  47.1 us
    another operation x5, other arithmetic, spd_solve(): return jax.scipy.linalg.cho_solve((chol_lower, True), right_side.T).T  39.7 us
    reduce_scatter x1, waiting for transfers between devices, body(): lax.psum_scatter(partial, 'item', scatter_dimension=0, tiled=True)  31.8 us
  transfers between devices with their start and end apart: 6, of which 5 were waited for; matrix products, arithmetic and copies ran while one was open for 21% of the time, Pallas kernels for 0%

profile of v1, /device:TPU:1, one launch (start us, length us, event | category | flops | bytes accessed | tf_op | source)
XLA Modules:
  0.0 606.3 jit_solution(13550863670987385643)
XLA Ops:
  9.6 114.9 %all-gather.3.cloned.1.call-done = bf16[32768,256]{1,0:T(8,128)(2,1)} async-done(((bf16[2048,256]{1,0:T(8,128)(2,1)}), bf16[32768,256]{1,0:T(8,128)(2,1)}) %all-gather.3.cloned.1.call-update) | async-done | bytes 16777232 | tf_op jit(solution)/shard_map/all_gather | solution.py:36
  124.5 8.5 %gather_fusion = bf16[64,128,256]{2,1,0:T(8,128)(2,1)} fusion(bf16[256,128,256]{2,1,0:T(8,128)(2,1)} %bitcast.145, s32[1024]{0:T(1024)S(1)} %pad_clamp_fusion), kind=kCustom, calls=%fused_computation | custom fusion | bytes 8388864 | tf_op jit(solution)/shard_map/gather | solution.py:37
  133.0 6.7 %fusion = f32[16,256,256]{1,2,0:T(8,128)} fusion(bf16[16,4,128,256]{3,2,1,0:T(8,128)(2,1)} %bitcast.142, bf16[16,4,256,128]{3,2,1,0:T(8,128)(2,1)} %param.7, pred[16,256]{1,0:T(8,128)(4,1)S(1)} %iota_compare_fusion.5), kind=kOutput, calls=%fused_computation.7 | convolution fusion | flops 1074790400 | bytes 12587008 | tf_op jit(solution)/shard_map/ksrt,kstc->krc/dot_general | solution.py:39
  142.9 31.8 %reduce-scatter.3.cloned.1.call-done = f32[2,256,256]{1,2,0:T(8,128)} async-done(((f32[16,256,256]{1,2,0:T(8,128)}), f32[2,256,256]{1,2,0:T(8,128)}) %reduce-scatter.3.cloned.1.call-update) | async-done | bytes 524304 | tf_op jit(solution)/shard_map/reduce_scatter | solution.py:43
  174.7 2.2 multiply_reduce_fusion
  186.9 1.4 fusion.46
  188.3 2.2 convolution_bitcast_fusion
  190.6 61.9 %all-reduce.8.cloned.1.call-done = (f32[256,256]{1,0:T(8,128)}, f32[256,256]{0,1:T(8,128)}, f32[256,256]{0,1:T(8,128)}) async-done(((f32[256,256]{1,0:T(8,128)}, f32[256,256]{0,1:T(8,128)}, f32[256,256]{0,1:T(8,128)}), (f32[256,256]{1,0:T(8,128)}, f32[256,256]{0,1:T(8,128)}, f32[256,256]{0,1:T(8,128)})) %all-reduce.8.cloned.1.call-update) | async-done | bytes 786448 | tf_op jit(solution)/shard_map/psum | solution.py:50
  253.1 89.9 %all-reduce.6.cloned.1.call-done = (f32[256,256]{0,1:T(8,128)}, f32[256,256]{0,1:T(8,128)}, f32[256,256]{0,1:T(8,128)}) async-done(((f32[256,256]{0,1:T(8,128)}, f32[256,256]{0,1:T(8,128)}, f32[256,256]{0,1:T(8,128)}), (f32[256,256]{0,1:T(8,128)}, f32[256,256]{0,1:T(8,128)}, f32[256,256]{0,1:T(8,128)})) %all-reduce.6.cloned.1.call-update) | async-done | bytes 786448 | tf_op jit(solution)/shard_map/psum | solution.py:51
  344.3 11.7 %cholesky.130 = f32[128,128]{1,0:T(8,128)S(1)} custom-call(f32[128,128]{1,0:T(8,128)S(1)} %cholesky.194), custom_call_target="Cholesky" | custom-call | tf_op jit(solution)/shard_map/jit(cholesky)/cholesky | solution.py:21
  356.1 9.8 %custom-call.25 = f32[1,128,128]{1,2,0:T(8,128)S(1)} custom-call(f32[1,128,128]{2,1,0:T(8,128)S(1)} %get-tuple-element.62), custom_call_target="InvertDiagBlocksLowerTriangular" | custom-call | tf_op jit(solution)/shard_map/jit(cholesky)/cholesky | solution.py:21
  366.4 11.7 %cholesky.147 = f32[128,128]{1,0:T(8,128)S(1)} custom-call(f32[128,128]{1,0:T(8,128)S(1)} %convolution_subtract_fusion.5), custom_call_target="Cholesky" | custom-call | tf_op jit(solution)/shard_map/jit(cholesky)/cholesky | solution.py:21
  380.3 4.3 while.2
  381.1 1.4 bitcast_dynamic-update-slice_fusion.4
  383.2 1.4 bitcast_dynamic-update-slice_fusion.4
  384.6 19.7 %custom-call.22 = f32[2,128,128]{1,2,0:T(8,128)S(1)} custom-call(f32[2,128,128]{2,1,0:T(8,128)S(1)} %get-tuple-element.11), custom_call_target="InvertDiagBlocksLowerTriangular" | custom-call | tf_op jit(solution)/shard_map/jit(_cho_solve)/triangular_solve | solution.py:22
  406.4 3.6 select_convert_fusion
  410.0 3.2 convert_bitcast_fusion
  413.2 6.8 %copy.78 = bf16[8,8,128,256]{3,1,2,0:T(8,128)(2,1)} copy(bf16[8,8,128,256]{2,3,1,0:T(8,128)(2,1)} %bitcast.143) | data formatting | bytes 8388608
  420.0 10.2 %convolution_convert_fusion = bf16[256,32768]{1,0:T(8,128)(2,1)} fusion(bf16[64,32768]{1,0:T(8,128)(2,1)} %bitcast.144, s32[64]{0:T(128)S(1)} %eq.15), kind=kOutput, calls=%fused_computation.5 | convolution fusion | flops 1082146816 | bytes 20971776 | tf_op jit(solution)/shard_map/dot_general | solution.py:67
  430.2 25.6 %convert_element_type.26 = bf16[32768,256]{1,0:T(8,128)(2,1)} reshape(bf16[256,32768]{1,0:T(8,128)(2,1)} %convolution_convert_fusion) | data formatting | bytes 33554432 | tf_op jit(solution)/shard_map/convert_element_type | solution.py:69
  455.9 21.4 %copy.58 = bf16[32768,256]{0,1:T(8,128)(2,1)} copy(bf16[32768,256]{1,0:T(8,128)(2,1)} %convert_element_type.26) | data formatting | bytes 33554432 | tf_op jit(solution)/shard_map/convert_element_type | solution.py:69
  479.0 11.7 %cholesky.164 = f32[128,128]{1,0:T(8,128)S(1)} custom-call(f32[128,128]{1,0:T(8,128)S(1)} %cholesky.197), custom_call_target="Cholesky" | custom-call | tf_op jit(solution)/shard_map/jit(cholesky)/cholesky | solution.py:21
  490.7 9.8 %custom-call.26 = f32[1,128,128]{1,2,0:T(8,128)S(1)} custom-call(f32[1,128,128]{2,1,0:T(8,128)S(1)} %get-tuple-element.58), custom_call_target="InvertDiagBlocksLowerTriangular" | custom-call | tf_op jit(solution)/shard_map/jit(cholesky)/cholesky | solution.py:21
  501.1 11.7 %cholesky.181 = f32[128,128]{1,0:T(8,128)S(1)} custom-call(f32[128,128]{1,0:T(8,128)S(1)} %convolution_subtract_fusion.4), custom_call_target="Cholesky" | custom-call | tf_op jit(solution)/shard_map/jit(cholesky)/cholesky | solution.py:21
  515.5 4.0 while.3
  516.1 1.4 bitcast_dynamic-update-slice_fusion.5
  519.5 19.9 %custom-call.23 = f32[2,128,128]{1,2,0:T(8,128)S(1)} custom-call(f32[2,128,128]{2,1,0:T(8,128)S(1)} %get-tuple-element.19), custom_call_target="InvertDiagBlocksLowerTriangular" | custom-call | tf_op jit(solution)/shard_map/jit(_cho_solve)/triangular_solve | solution.py:22
  539.4 49.7 %reduce-scatter.5.cloned.1.call-done = bf16[2048,256]{0,1:T(8,128)(2,1)} async-done(((bf16[32768,256]{0,1:T(8,128)(2,1)}), bf16[2048,256]{0,1:T(8,128)(2,1)}) %reduce-scatter.5.cloned.1.call-update) | async-done | bytes 1048592 | tf_op jit(solution)/shard_map/reduce_scatter | solution.py:68
  589.1 1.7 fusion.8
  590.8 2.1 convolution_subtract_fusion.1
  597.2 1.8 copy.60
  (102 shorter events, 32.2 us)
Async XLA Ops:
  7.2 167.5 %copy-start = (f32[256,256]{1,0:T(8,128)S(1)}, f32[256,256]{1,0:T(8,128)}, u32[]{:S(2)}) copy-start(f32[256,256]{1,0:T(8,128)} %param.11) | copy-start | bytes 786436
  7.2 117.4 %all-gather.3.cloned.1.call-start = ((), (), s32[]{:S(2)}) async-start(), calls=%async_computation.2 | async-start | bytes 17825792 | tf_op jit(solution)/shard_map/all_gather | solution.py:36
  7.9 166.8 %reduce-scatter.3.cloned.1.call-start = ((), (), s32[]{:S(2)}) async-start(), calls=%async_computation.3 | async-start | bytes 4718592 | tf_op jit(solution)/shard_map/reduce_scatter | solution.py:43
  139.8 0.7 copy-start.7
  139.8 1.9 copy-start.4
  139.8 112.7 %all-reduce.8.cloned.1.call-start = ((), (), s32[]{:S(2)}) async-start(), calls=%async_computation.7 | async-start | bytes 1572864 | tf_op jit(solution)/shard_map/psum | solution.py:50
  183.4 4.9 copy-start.3
  190.6 152.5 %all-reduce.6.cloned.1.call-start = ((), (), s32[]{:S(2)}) async-start(), calls=%async_computation.6 | async-start | bytes 1572864 | tf_op jit(solution)/shard_map/psum | solution.py:51
  252.5 153.8 %all-gather.5.cloned.1.call-start = ((), (), s32[]{:S(2)}) async-start(), calls=%async_computation.4 | async-start | bytes 2359296 | tf_op jit(solution)/shard_map/all_gather | solution.py:52
  253.1 336.0 %reduce-scatter.5.cloned.1.call-start = ((), (), s32[]{:S(2)}) async-start(), calls=%async_computation.5 | async-start | bytes 17825792 | tf_op jit(solution)/shard_map/reduce_scatter | solution.py:68
  343.0 61.3 %copy-start.6 = (f32[256,256]{0,1:T(8,128)S(1)}, f32[256,256]{0,1:T(8,128)}, u32[]{:S(2)}) copy-start(f32[256,256]{0,1:T(8,128)} %get-tuple-element.45) | copy-start | bytes 786436
  406.3 3.7 copy-start.2
  477.3 1.0 copy-start.5
  596.0 3.0 copy-start.1
Sparse Core Ops, SparseCore 0:
  10.1 114.3 all-gather.2
  139.9 34.6 reduce-scatter.2
  190.7 61.7 all-reduce.7
  255.9 87.0 all-reduce.5
  345.2 26.7 all-gather.4
  477.5 111.6 reduce-scatter.4

commit v2 on v1

v2 whole, which is shorter than its diff:
```python
import functools

import jax
import jax.numpy as jnp
from jax import lax
from jax.experimental import pallas as pl
from jax.experimental.pallas import tpu as pltpu
from jax.sharding import PartitionSpec as P

NS_STEPS = 6
HIGHEST = lax.Precision.HIGHEST
EPSILON = 1e-06
F32, BF16 = jnp.float32, jnp.bfloat16
VMEM = pl.BlockSpec(memory_space=pltpu.VMEM)


def send(src, dst, send_sem, recv_sem, **peer):
    return pltpu.make_async_remote_copy(
        src_ref=src,
        dst_ref=dst,
        send_sem=send_sem,
        recv_sem=recv_sem,
        device_id=peer,
        device_id_type=pl.DeviceIdType.MESH,
    )


def places():
    user, item = lax.axis_index("user"), lax.axis_index("item")
    return user // 4, user % 4, item // 2, item % 2, item


def y_peer(y, z, d):
    return ((y + d) % 4) * 4 + z


def z_peer(y, z, d):
    return y * 4 + (z + d) % 4


def greet(y, z, item):
    barrier = pltpu.get_barrier_semaphore()
    for d in range(1, 8):
        pl.semaphore_signal(
            barrier, inc=1, device_id={"item": (item + d) % 8}, device_id_type=pl.DeviceIdType.MESH
        )
    for d in range(1, 4):
        for peer in (y_peer(y, z, d), z_peer(y, z, d)):
            pl.semaphore_signal(
                barrier, inc=1, device_id={"user": peer}, device_id_type=pl.DeviceIdType.MESH
            )
    pl.semaphore_wait(barrier, 13)


def split(a):
    high = a.astype(BF16)
    return high, (a - high.astype(F32)).astype(BF16)


def dot3(a, b, dims):
    contract = ((dims[0],), (dims[1],)), ((), ())
    one = functools.partial(lax.dot_general, dimension_numbers=contract, preferred_element_type=F32)
    return one(a[0], b[0]) + (one(a[0], b[1]) + one(a[1], b[0]))


def rows_of(j):
    return pl.ds(pl.multiple_of(j * 32, 32), 32)


def scatter_start(term, buf, sems, base, item):
    copies = []
    for d in range(1, 8):
        j = (item + d) % 8
        copies.append(
            send(term.at[rows_of(j)], buf.at[item], sems[0].at[base + d], sems[1].at[base + d], item=j)
        )
        copies[-1].start()
    buf[item] = term[rows_of(item)]
    return copies


def share_start(buf, sems, base, at, peer_of, value):
    buf[at] = value
    copies = []
    for d in range(1, 4):
        copies.append(
            send(buf.at[at], buf.at[at], sems[0].at[base + d], sems[1].at[base + d], user=peer_of(d))
        )
        copies[-1].start()
    return copies


def gather_start(full, sems, base, item, value):
    full[rows_of(item)] = value
    copies = []
    for d in range(1, 8):
        part = full.at[rows_of(item)]
        copies.append(
            send(part, part, sems[0].at[base + d], sems[1].at[base + d], item=(item + d) % 8)
        )
        copies[-1].start()
    return copies


def arrive(copies):
    for copy in copies:
        copy.wait_recv()


def total_of(buf, count):
    total = buf[0]
    for n in range(1, count):
        total = total + buf[n]
    return total


def sum_kernel(term, weights, full, all_weights, buf_x, buf_y, buf_z, send_sem, recv_sem):
    sems = (send_sem, recv_sem)
    y, z, _, _, item = places()
    all_weights[y, z] = weights[...]
    greet(y, z, item)
    started = scatter_start(term, buf_x, sems, 0, item)
    wide = []
    for d in range(1, 4):
        mine = all_weights.at[y, z]
        wide.append(
            send(mine, mine, send_sem.at[24 + d], recv_sem.at[24 + d], user=y_peer(y, z, d))
        )
        wide[-1].start()
    arrive(started)
    step = share_start(
        buf_y, sems, 8, y, functools.partial(y_peer, y, z), total_of(buf_x, 8)
    )
    arrive(wide)
    for d in range(1, 4):
        mine = all_weights.at[:, z]
        wide.append(
            send(mine, mine, send_sem.at[28 + d], recv_sem.at[28 + d], user=z_peer(y, z, d))
        )
        wide[-1].start()
    arrive(step)
    started += step
    step = share_start(
        buf_z, sems, 12, z, functools.partial(z_peer, y, z), total_of(buf_y, 4)
    )
    arrive(step)
    started += step
    step = gather_start(full, sems, 16, item, total_of(buf_z, 4))
    arrive(step)
    arrive(wide[3:])
    for copy in started + step + wide:
        copy.wait_send()


def sum_everywhere(term, weights):
    return pl.pallas_call(
        sum_kernel,
        out_shape=(
            jax.ShapeDtypeStruct((256, 256), F32),
            jax.ShapeDtypeStruct((4, 4, 16, 256), F32),
        ),
        in_specs=[VMEM, VMEM],
        out_specs=(VMEM, VMEM),
        scratch_shapes=[
            pltpu.VMEM((8, 32, 256), F32),
            pltpu.VMEM((4, 32, 256), F32),
            pltpu.VMEM((4, 32, 256), F32),
            pltpu.SemaphoreType.DMA((32,)),
            pltpu.SemaphoreType.DMA((32,)),
        ],
        compiler_params=pltpu.CompilerParams(collective_id=0, has_side_effects=True),
        name="sum_everywhere",
    )(term, weights)


def mid_kernel(
    partial,
    weights,
    time_factor,
    inner_inv,
    weight_gram,
    polar_all,
    slices,
    new_time,
    item_gram,
    recv1,
    outgoing,
    relay,
    recv2,
    scaled,
    iterate,
    term,
    full,
    buf_x,
    buf_y,
    buf_z,
    send_sem,
    recv_sem,
):
    sems = (send_sem, recv_sem)
    y, z, x, core, item = places()
    partner = x * 2 + (1 - core)
    right, left = ((x + 1) % 4) * 2 + core, ((x + 3) % 4) * 2 + core
    done = []

    def go(src, dst, n, **peer):
        copy = send(src, dst, send_sem.at[n], recv_sem.at[n], **peer)
        copy.start()
        done.append(copy)
        return copy

    greet(y, z, item)

    def share(d):
        return (((x + d) % 4) * 2 + core) * 2

    def other_share(d):
        return (((x + d) % 4) * 2 + (1 - core)) * 2

    cross = {}
    for d in (2, 1, 3, 0):
        cross[d] = go(partial.at[pl.ds(other_share(d), 2)], recv1.at[d], d, item=partner)
    cross[2].wait_recv()
    outgoing[0] = (partial[share(2)] + recv1[2, 0]).astype(BF16)
    far_right = go(outgoing.at[0], relay.at[0], 4, item=right)
    outgoing[1] = (partial[share(2) + 1] + recv1[2, 1]).astype(BF16)
    far_left = go(outgoing.at[1], relay.at[1], 5, item=left)
    cross[1].wait_recv()
    outgoing[3] = (partial[share(1) + 1] + recv1[1, 1]).astype(BF16)
    near_right = go(outgoing.at[3], recv2.at[0], 6, item=right)
    cross[3].wait_recv()
    outgoing[4] = (partial[share(3)] + recv1[3, 0]).astype(BF16)
    near_left = go(outgoing.at[4], recv2.at[1], 7, item=left)
    far_right.wait_recv()
    outgoing[2] = (partial[share(1)] + recv1[1, 0] + relay[0].astype(F32)).astype(BF16)
    sum_right = go(outgoing.at[2], recv2.at[2], 8, item=right)
    far_left.wait_recv()
    outgoing[5] = (partial[share(3) + 1] + recv1[3, 1] + relay[1].astype(F32)).astype(BF16)
    sum_left = go(outgoing.at[5], recv2.at[3], 9, item=left)
    cross[0].wait_recv()
    for copy in (near_right, near_left, sum_right, sum_left):
        copy.wait_recv()
    factor = split(time_factor[...])
    for k, parts in enumerate(((2, 1), (0, 3))):
        projection = partial[share(0) + k] + recv1[0, k]
        for n in parts:
            projection = projection + recv2[n].astype(F32)
        projection = projection * weights[k]
        scaled[k] = projection
        target = dot3(split(projection), factor, (1, 1))
        norm = jnp.sum(target * target, axis=(0, 1), keepdims=True) + EPSILON
        iterate[k] = target / jnp.sqrt(norm)

    def sweep(_, carry):
        for k in range(2):
            now = iterate[k]
            parts = split(now)
            gram = dot3(parts, parts, (1, 1))
            iterate[k] = 1.5 * now - 0.5 * dot3(split(gram), parts, (1, 0))
        return carry

    lax.fori_loop(0, NS_STEPS, sweep, 0)
    total = None
    for k in range(2):
        polar = iterate[k]
        slices[k] = polar.astype(BF16)
        polar_all[item * 2 + k] = polar.astype(BF16)
        one = dot3(split(polar.T), split(scaled[k]), (1, 0))
        total = one if total is None else total + one
    term[...] = total
    step = scatter_start(term, buf_x, sems, 16, item)
    done.extend(step)
    mine = polar_all.at[pl.ds(item * 2, 2)]
    own_right = go(mine, mine, 48, item=right)
    own_left = go(mine, mine, 49, item=left)
    crossing = [go(mine, mine, 50, item=partner)]
    arrive(step)
    step = share_start(buf_y, sems, 24, y, functools.partial(y_peer, y, z), total_of(buf_x, 8))
    done.extend(step)
    arrive(step)
    step = share_start(buf_z, sems, 28, z, functools.partial(z_peer, y, z), total_of(buf_y, 4))
    done.extend(step)
    own_right.wait_recv()
    hop = polar_all.at[left * 2]
    hop_right = go(hop, hop, 51, item=right)
    own_left.wait_recv()
    hop = polar_all.at[right * 2 + 1]
    hop_left = go(hop, hop, 52, item=left)
    for n, source in ((53, left), (54, right)):
        block = polar_all.at[pl.ds(source * 2, 2)]
        crossing.append(go(block, block, n, item=partner))
    arrive(step)
    step = gather_start(full, sems, 32, item, total_of(buf_z, 4))
    done.extend(step)
    hop_right.wait_recv()
    hop_left.wait_recv()
    block = polar_all.at[pl.ds(share(2), 2)]
    crossing.append(go(block, block, 55, item=partner))
    arrive(step)
    raw = dot3(split(full[...]), split(inner_inv[...]), (1, 0))
    fresh = raw / jnp.sqrt(jnp.sum(raw * raw, axis=0, keepdims=True) + EPSILON)
    new_time[...] = fresh
    item_gram[...] = dot3(split(fresh.T), split(fresh), (1, 0)) * weight_gram[...]
    arrive(crossing)
    for copy in done:
        copy.wait_send()


def middle(partial, weights, time_factor, inner_inv, weight_gram):
    return pl.pallas_call(
        mid_kernel,
        out_shape=(
            jax.ShapeDtypeStruct((16, 256, 256), BF16),
            jax.ShapeDtypeStruct((2, 256, 256), BF16),
            jax.ShapeDtypeStruct((256, 256), F32),
            jax.ShapeDtypeStruct((256, 256), F32),
        ),
        in_specs=[VMEM] * 5,
        out_specs=(VMEM,) * 4,
        scratch_shapes=[
            pltpu.VMEM((4, 2, 256, 256), F32),
            pltpu.VMEM((6, 256, 256), BF16),
            pltpu.VMEM((2, 256, 256), BF16),
            pltpu.VMEM((4, 256, 256), BF16),
            pltpu.VMEM((2, 256, 256), F32),
            pltpu.VMEM((2, 256, 256), F32),
            pltpu.VMEM((256, 256), F32),
            pltpu.VMEM((256, 256), F32),
            pltpu.VMEM((8, 32, 256), F32),
            pltpu.VMEM((4, 32, 256), F32),
            pltpu.VMEM((4, 32, 256), F32),
            pltpu.SemaphoreType.DMA((56,)),
            pltpu.SemaphoreType.DMA((56,)),
        ],
        compiler_params=pltpu.CompilerParams(collective_id=1, has_side_effects=True),
        name="middle",
    )(partial, weights, time_factor, inner_inv, weight_gram)


def spd_inverse(gram):
    lower = jnp.linalg.cholesky(gram)
    return jax.scipy.linalg.cho_solve((lower, True), jnp.eye(gram.shape[0], dtype=F32))


def body(tile_values, tile_ids, lengths, user_weights, time_factor, item_factor):
    user_count = lax.axis_size("user")
    item_count = lax.axis_size("item")
    item_pos = lax.axis_index("item")
    users_here, slots_user, time_rows, tile_width = tile_values.shape
    rank_size = time_factor.shape[0]
    tiles_owned = item_factor.shape[0] // tile_width
    slot_count = users_here * slots_user
    share_count = users_here // item_count
    flat_ids = (tile_ids - item_pos * (tiles_owned * user_count)).reshape(slot_count)
    live = jnp.arange(time_rows, dtype=jnp.int32)[None, :] < lengths[:, None]
    shard_rows = lax.all_gather(item_factor, "user", axis=0, tiled=True)
    item_term = lax.dot_general(
        item_factor, item_factor, (((0,), (0,)), ((), ())), preferred_element_type=F32
    )
    item_inner, all_weights = sum_everywhere(item_term, user_weights)
    all_weights = all_weights.reshape(user_count * users_here, rank_size)
    weight_gram = jnp.dot(all_weights.T, all_weights, precision=HIGHEST)
    inner_inv = spd_inverse(item_inner * weight_gram)
    panels = shard_rows.reshape(tiles_owned * user_count, tile_width, rank_size)[flat_ids]
    panels = panels.reshape(users_here, slots_user, tile_width, rank_size)
    partial = jnp.einsum("ksrt,kstc->krc", tile_values, panels, preferred_element_type=F32)
    partial = jnp.where(live[:, :, None], partial, 0.0)
    share_weights = lax.dynamic_slice_in_dim(user_weights, item_pos * share_count, share_count, 0)
    polar_all, slices, new_time, item_gram = middle(
        partial, share_weights[:, None, :], time_factor, inner_inv, weight_gram
    )
    gram_inv = spd_inverse(item_gram)
    user_maps = (
        jnp.einsum("krc,cd->krd", polar_all.astype(F32), new_time, precision=HIGHEST)
        * user_weights[:, None, :]
    )
    user_maps = jnp.where(live[:, :, None], user_maps, 0.0).astype(BF16)
    tile_terms = jnp.einsum(
        "ksrt,krc->kstc", tile_values, user_maps, preferred_element_type=F32
    ).astype(BF16)
    tile_terms = tile_terms.reshape(slot_count, tile_width * rank_size)
    row_count = tiles_owned * tile_width * user_count
    wanted = jnp.arange(row_count // tile_width, dtype=jnp.int32)
    hits = (flat_ids[None, :] == wanted[:, None]).astype(BF16)
    summed = jnp.dot(hits, tile_terms, preferred_element_type=F32)
    item_mttkrp = lax.psum_scatter(
        summed.reshape(row_count, rank_size).astype(BF16), "user", scatter_dimension=0, tiled=True
    ).astype(F32)
    new_items = jnp.dot(item_mttkrp, gram_inv, precision=HIGHEST)
    return (slices, new_time, new_items)


def solution(mesh):
    in_specs = (
        P("user", "item", None, None),
        P("user", "item"),
        P("user"),
        P("user", None),
        P(),
        P(("item", "user"), None),
    )
    out_specs = (P(("user", "item"), None, None), P(), P(("item", "user"), None))
    return jax.shard_map(body, mesh=mesh, in_specs=in_specs, out_specs=out_specs, check_vma=False)
```

time: 618 us -> 375 us (0.61); the launches traced: 606 us -> 370 us
  waiting for transfers between devices: 349 us -> 64.7 us
  Pallas kernels: 0 us -> 79.2 us
  local copies, waits for them, and re-layouts: 74.3 us -> 54.1 us
  matrix products: 53 us -> 44.7 us
    psum x2 -> x0, waiting for transfers between devices: 152 us -> none  [the longest x1 89.9 us: body(): time_mttkrp, weight_gram, item_inner = lax.psum(sums, 'user')]
    all_gather x1, waiting for transfers between devices: 115 us -> 19 us  [body(): shard_rows = lax.all_gather(item_factor, 'user', axis=0, tiled=True)]
    pallas_call x0 -> x2, Pallas kernels: none -> 79.2 us  [the longest x1 49.2 us: middle(): pl.pallas_call(mid_kernel, out_shape=(jax.ShapeDtypeStruct((16, 256, 256)...]
    reduce_scatter x2 -> x1, waiting for transfers between devices: 81.5 us -> 45 us  [body(): lax.psum_scatter(summed.reshape(row_count, rank_size).astype(BF16), 'user...]
    convert_element_type x2 -> x1, local copies, waits for them, and re-layouts: 47.1 us -> 25.6 us  [body(): summed.reshape(row_count, rank_size).astype(BF16)]
    another operation x16, matrix products: 10.6 us -> 4.36 us  [the longest x12 3.41 us: spd_inverse(): jax.scipy.linalg.cho_solve((lower, True), jnp.eye(gram.shape[0], dtype=F32))]
    dot_general x19 -> x5, matrix products: 32.4 us -> 31.2 us  [the longest x1 19.4 us: body(): summed = jnp.dot(hits, tile_terms, preferred_element_type=F32)]
    another operation x18 -> x19, other arithmetic: 108 us -> 109 us  [the longest x13 68.8 us: spd_inverse(): lower = jnp.linalg.cholesky(gram)]
  transfers between devices with their start and end apart: 6 -> 2, of which waited for: 5 -> 2; matrix products, arithmetic and copies ran while one was open for 21% -> 35% of each run, Pallas kernels for 0% -> 8%
where the time goes in v2:
time: 375 us; the launch traced here: 370 us
  other arithmetic  110 us (29%)
  Pallas kernels  79.2 us (21%)
  waiting for transfers between devices  64.7 us (17%)
  local copies, waits for them, and re-layouts  54.1 us (14%)
  matrix products  44.7 us (12%)
  between operations  17.2 us (5%)
    another operation x13, other arithmetic, spd_inverse(): lower = jnp.linalg.cholesky(gram)  68.8 us
    pallas_call x1, Pallas kernels, middle(): pl.pallas_call(mid_kernel, out_shape=(jax.ShapeDtypeStruct((16, 256, 256)...  49.2 us
    reduce_scatter x1, waiting for transfers between devices, body(): lax.psum_scatter(summed.reshape(row_count, rank_size).astype(BF16), 'user...  45 us
    another operation x6, other arithmetic, spd_inverse(): jax.scipy.linalg.cho_solve((lower, True), jnp.eye(gram.shape[0], dtype=F32))  40.3 us
    pallas_call x1, Pallas kernels, sum_everywhere(): pl.pallas_call(sum_kernel, out_shape=(jax.ShapeDtypeStruct((256, 256), F3...  30 us
    convert_element_type x1, local copies, waits for them, and re-layouts, body(): summed.reshape(row_count, rank_size).astype(BF16)  25.6 us
    dot_general x1, matrix products, body(): summed = jnp.dot(hits, tile_terms, preferred_element_type=F32)  19.4 us
    all_gather x1, waiting for transfers between devices, body(): shard_rows = lax.all_gather(item_factor, 'user', axis=0, tiled=True)  19 us
  transfers between devices with their start and end apart: 2, of which 2 were waited for; matrix products, arithmetic and copies ran while one was open for 35% of the time, Pallas kernels for 8%

profile of v2, /device:TPU:1, one launch (start us, length us, event | category | flops | bytes accessed | tf_op | source)
XLA Modules:
  0.0 370.1 jit_solution(3836342096696969566)
XLA Ops:
  8.9 0.7 constant_dynamic-slice_fusion.2
  10.2 2.8 fusion.35.term
  13.0 30.0 %sum_everywhere.1 = (f32[256,256]{1,0:T(8,128)}, f32[4,4,16,256]{3,2,1,0:T(8,128)}) custom-call(f32[256,256]{1,0:T(8,128)} %fusion.35.term, f32[16,256]{1,0:T(8,128)} %weights.1), custom_call_target="tpu_custom_call" | custom-call | tf_op jit(solution)/shard_map/sum_everywhere/pallas_call | solution.py:156
  43.0 1.1 copy.20
  44.1 1.6 convolution_bitcast_fusion.weight_gram
  46.1 11.7 %cholesky.130 = f32[128,128]{1,0:T(8,128)S(1)} custom-call(f32[128,128]{1,0:T(8,128)S(1)} %cholesky.194), custom_call_target="Cholesky" | custom-call | tf_op jit(solution)/shard_map/jit(cholesky)/cholesky | solution.py:341
  57.9 9.8 %custom-call.15 = f32[1,128,128]{1,2,0:T(8,128)S(1)} custom-call(f32[1,128,128]{2,1,0:T(8,128)S(1)} %get-tuple-element.60), custom_call_target="InvertDiagBlocksLowerTriangular" | custom-call | tf_op jit(solution)/shard_map/jit(cholesky)/cholesky | solution.py:341
  68.2 11.7 %cholesky.147 = f32[128,128]{1,0:T(8,128)S(1)} custom-call(f32[128,128]{1,0:T(8,128)S(1)} %convolution_subtract_fusion.5), custom_call_target="Cholesky" | custom-call | tf_op jit(solution)/shard_map/jit(cholesky)/cholesky | solution.py:341
  82.2 3.8 %while.4 = (s32[]{:T(128)}, f32[256,256]{1,0:T(8,128)S(1)}, s32[2,2]{1,0:T(2,128)S(1)}, f32[2,128,128]{2,1,0:T(8,128)S(1)}, s32[]{:T(128)}) while((s32[]{:T(128)}, f32[256,256]{1,0:T(8,128)S(1)}, s32[2,2]{1,0:T(2,128)S(1)}, f32[2,128,128]{2,1,0:T(8,128)S(1)}, s32[]{:T(128)}) %tuple.47), condition=%wide.while_cond, body=%wide.while_body.sunk | while | flops 2 | bytes 131189 | solution.py:342
  82.8 1.3 bitcast_dynamic-update-slice_fusion.4
  84.7 1.3 bitcast_dynamic-update-slice_fusion.4
  86.0 19.7 %custom-call.16 = f32[2,128,128]{1,2,0:T(8,128)S(1)} custom-call(f32[2,128,128]{2,1,0:T(8,128)S(1)} %get-tuple-element.31), custom_call_target="InvertDiagBlocksLowerTriangular" | custom-call | tf_op jit(solution)/shard_map/jit(_cho_solve)/triangular_solve | solution.py:342
  107.5 0.7 pad_maximum_fusion.inner_inv
  108.3 19.0 %all-gather.2.cloned.1.call-done = bf16[32768,256]{1,0:T(8,128)(2,1)} async-done(((bf16[2048,256]{1,0:T(8,128)(2,1)}), bf16[32768,256]{1,0:T(8,128)(2,1)}) %all-gather.2.cloned.1.call-update) | async-done | bytes 16777232 | tf_op jit(solution)/shard_map/all_gather | solution.py:356
  127.3 8.5 %gather_fusion = bf16[64,128,256]{2,1,0:T(8,128)(2,1)} fusion(bf16[256,128,256]{2,1,0:T(8,128)(2,1)} %bitcast.114, s32[1024]{0:T(1024)S(1)} %pad_clamp_fusion), kind=kCustom, calls=%fused_computation | custom fusion | bytes 8388864 | tf_op jit(solution)/shard_map/gather | solution.py:364
  135.8 5.9 %fusion.partial = f32[16,256,256]{2,1,0:T(8,128)} fusion(bf16[16,4,256,128]{3,2,1,0:T(8,128)(2,1)} %param.9, bf16[16,4,128,256]{3,2,1,0:T(8,128)(2,1)} %bitcast.111, pred[16,256]{1,0:T(8,128)(4,1)S(1)} %iota_compare_fusion.6), kind=kOutput, calls=%fused_computation.7 | convolution fusion | flops 1074790400 | bytes 12587008 | tf_op jit(solution)/shard_map/ksrt,kstc->krc/dot_general | solution.py:366
  141.7 49.2 %middle.1 = (bf16[16,256,256]{2,1,0:T(8,128)(2,1)}, bf16[2,256,256]{2,1,0:T(8,128)(2,1)}, f32[256,256]{1,0:T(8,128)}, f32[256,256]{1,0:T(8,128)}) custom-call(f32[16,256,256]{2,1,0:T(8,128)} %fusion.partial, f32[2,1,256]{2,1,0:T(1,128)} %broadcast_in_dim.31.weights, f32[256,256]{1,0:T(8,128)} %time_factor.1, f32[256,256]{1,0:T(8,128)} %pad_maximum_fusion.inner_inv, ...), custom_call_target="tpu_custom_call" | custom-call | tf_op jit(solution)/shard_map/middle/pallas_call | solution.py:310
  190.9 3.8 %select_convert_fusion = bf16[16,256,256]{1,2,0:T(8,128)(2,1)S(1)} fusion(bf16[16,256,256]{2,1,0:T(8,128)(2,1)} %get-tuple-element.15, f32[16,256]{1,0:T(8,128)S(1)} %copy-done.5, pred[16,256]{1,0:T(8,128)(4,1)S(1)} %iota_compare_fusion.6, f32[256,256]{1,0:T(8,128)} %get-tuple-element.159), kind=kOutput, calls=%fused_computation.9 | convolution fusion | flops 3224371200 | bytes 4476928 | tf_op jit(solution)/shard_map/krc,cd->krd/dot_general | solution.py:374
  194.7 3.2 convert_bitcast_fusion
  198.0 6.7 %copy.30 = bf16[8,8,128,256]{3,1,2,0:T(8,128)(2,1)} copy(bf16[8,8,128,256]{2,3,1,0:T(8,128)(2,1)} %bitcast.112) | data formatting | bytes 8388608
  204.7 19.4 %convolution_convert_fusion = bf16[256,32768]{1,0:T(8,128)(2,1)} fusion(bf16[64,32768]{1,0:T(8,128)(2,1)} %bitcast.113, s32[64]{0:T(128)S(1)} %eq.22), kind=kOutput, calls=%fused_computation.5 | convolution fusion | flops 1082146816 | bytes 20971776 | tf_op jit(solution)/shard_map/dot_general | solution.py:385
  224.1 25.6 %convert_element_type.29 = bf16[32768,256]{1,0:T(8,128)(2,1)} reshape(bf16[256,32768]{1,0:T(8,128)(2,1)} %convolution_convert_fusion) | data formatting | bytes 33554432 | tf_op jit(solution)/shard_map/convert_element_type | solution.py:387
  249.7 0.9 copy-done.2
  250.9 11.7 %cholesky.164 = f32[128,128]{1,0:T(8,128)S(1)} custom-call(f32[128,128]{1,0:T(8,128)S(1)} %cholesky.197), custom_call_target="Cholesky" | custom-call | tf_op jit(solution)/shard_map/jit(cholesky)/cholesky | solution.py:341
  262.6 9.8 %custom-call.17 = f32[1,128,128]{1,2,0:T(8,128)S(1)} custom-call(f32[1,128,128]{2,1,0:T(8,128)S(1)} %get-tuple-element.56), custom_call_target="InvertDiagBlocksLowerTriangular" | custom-call | tf_op jit(solution)/shard_map/jit(cholesky)/cholesky | solution.py:341
  272.9 11.7 %cholesky.181 = f32[128,128]{1,0:T(8,128)S(1)} custom-call(f32[128,128]{1,0:T(8,128)S(1)} %convolution_subtract_fusion.4), custom_call_target="Cholesky" | custom-call | tf_op jit(solution)/shard_map/jit(cholesky)/cholesky | solution.py:341
  287.3 4.0 %while.5 = (s32[]{:T(128)}, f32[256,256]{1,0:T(8,128)S(1)}, s32[2,2]{1,0:T(2,128)S(1)}, f32[2,128,128]{2,1,0:T(8,128)S(1)}, s32[]{:T(128)}) while((s32[]{:T(128)}, f32[256,256]{1,0:T(8,128)S(1)}, s32[2,2]{1,0:T(2,128)S(1)}, f32[2,128,128]{2,1,0:T(8,128)S(1)}, s32[]{:T(128)}) %tuple.59), condition=%wide.while_cond.clone, body=%wide.while_body.clone.sunk | while | flops 2 | bytes 131189 | solution.py:342
  287.9 1.4 bitcast_dynamic-update-slice_fusion.5
  289.9 1.4 bitcast_dynamic-update-slice_fusion.5
  291.3 19.9 %custom-call.18 = f32[2,128,128]{1,2,0:T(8,128)S(1)} custom-call(f32[2,128,128]{2,1,0:T(8,128)S(1)} %get-tuple-element.32), custom_call_target="InvertDiagBlocksLowerTriangular" | custom-call | tf_op jit(solution)/shard_map/jit(_cho_solve)/triangular_solve | solution.py:342
  313.0 45.0 %reduce-scatter.2.cloned.1.call-done = bf16[2048,256]{1,0:T(8,128)(2,1)} async-done(((bf16[32768,256]{1,0:T(8,128)(2,1)}), bf16[2048,256]{1,0:T(8,128)(2,1)}) %reduce-scatter.2.cloned.1.call-update) | async-done | bytes 1048592 | tf_op jit(solution)/shard_map/reduce_scatter | solution.py:386
  358.0 3.6 fusion.2
  (75 shorter events, 13.6 us)
Async XLA Ops:
  7.2 120.1 %all-gather.2.cloned.1.call-start = ((), (), s32[]{:S(2)}) async-start(), calls=%async_computation.1 | async-start | bytes 17825792 | tf_op jit(solution)/shard_map/all_gather | solution.py:356
  7.9 350.1 %reduce-scatter.2.cloned.1.call-start = ((), (), s32[]{:S(2)}) async-start(), calls=%async_computation.2 | async-start | bytes 17825792 | tf_op jit(solution)/shard_map/reduce_scatter | solution.py:386
  45.7 62.5 %copy-start.1 = (f32[256,256]{1,0:T(8,128)}, f32[256,256]{1,0:T(8,128)S(1)}, u32[]{:S(2)}) copy-start(f32[256,256]{1,0:T(8,128)S(1)} %convolution_bitcast_fusion.weight_gram) | copy-start | bytes 786436
  45.7 62.5 %copy-start.6 = (s32[16]{0:T(128)S(1)}, s32[16]{0:T(128)}, u32[]{:S(2)}) copy-start(s32[16]{0:T(128)} %param.11) | copy-start | bytes 196
  141.7 49.2 %copy-start.5 = (f32[16,256]{1,0:T(8,128)S(1)}, f32[16,256]{1,0:T(8,128)}, u32[]{:S(2)}) copy-start(f32[16,256]{1,0:T(8,128)} %weights.1) | copy-start | bytes 49156
  190.9 3.9 %copy-start = (bf16[16,4,256,128]{3,2,1,0:T(8,128)(2,1)S(1)}, bf16[16,4,256,128]{3,2,1,0:T(8,128)(2,1)}, u32[]{:S(2)}) copy-start(bf16[16,4,256,128]{3,2,1,0:T(8,128)(2,1)} %param.9) | copy-start | bytes 12582916
  249.7 0.9 copy-start.2
  250.8 110.8 %copy-start.4 = (bf16[2,256,256]{2,1,0:T(8,128)(2,1)S(1)}, bf16[2,256,256]{2,1,0:T(8,128)(2,1)}, u32[]{:S(2)}) copy-start(bf16[2,256,256]{2,1,0:T(8,128)(2,1)} %get-tuple-element.158) | copy-start | bytes 786436
  272.4 89.8 %copy-start.3 = (f32[256,256]{1,0:T(8,128)S(1)}, f32[256,256]{1,0:T(8,128)}, u32[]{:S(2)}) copy-start(f32[256,256]{1,0:T(8,128)} %get-tuple-element.159) | copy-start | bytes 786436
Sparse Core Ops, SparseCore 0:
  10.1 117.1 all-gather.1
  249.8 108.1 reduce-scatter.1

commit v3 on v2

--- a/solution.py
+++ b/solution.py
@@ -114,12 +114,26 @@
     return total
 
 
-def sum_kernel(term, weights, full, all_weights, buf_x, buf_y, buf_z, send_sem, recv_sem):
+def sum_kernel(
+    term, weights, lists, full, all_weights, lists_y, lists_z, buf_x, buf_y, buf_z, send_sem, recv_sem
+):
     sems = (send_sem, recv_sem)
     y, z, _, _, item = places()
     all_weights[y, z] = weights[...]
+    lists_y[y] = lists[...]
+    lists_z[z] = lists[...]
     greet(y, z, item)
     started = scatter_start(term, buf_x, sems, 0, item)
+    names = []
+    for d in range(1, 4):
+        for n, held, at, peer in (
+            (32, lists_y, y, y_peer(y, z, d)),
+            (36, lists_z, z, z_peer(y, z, d)),
+        ):
+            names.append(
+                send(lists, held.at[at], send_sem.at[n + d], recv_sem.at[n + d], user=peer)
+            )
+            names[-1].start()
     wide = []
     for d in range(1, 4):
         mine = all_weights.at[y, z]
@@ -148,29 +162,32 @@
     step = gather_start(full, sems, 16, item, total_of(buf_z, 4))
     arrive(step)
     arrive(wide[3:])
-    for copy in started + step + wide:
+    arrive(names)
+    for copy in started + step + wide + names:
         copy.wait_send()
 
 
-def sum_everywhere(term, weights):
+def sum_everywhere(term, weights, lists):
     return pl.pallas_call(
         sum_kernel,
         out_shape=(
             jax.ShapeDtypeStruct((256, 256), F32),
             jax.ShapeDtypeStruct((4, 4, 16, 256), F32),
+            jax.ShapeDtypeStruct((4, 8, 128), jnp.int32),
+            jax.ShapeDtypeStruct((4, 8, 128), jnp.int32),
         ),
-        in_specs=[VMEM, VMEM],
-        out_specs=(VMEM, VMEM),
+        in_specs=[VMEM] * 3,
+        out_specs=(VMEM,) * 4,
         scratch_shapes=[
             pltpu.VMEM((8, 32, 256), F32),
             pltpu.VMEM((4, 32, 256), F32),
             pltpu.VMEM((4, 32, 256), F32),
-            pltpu.SemaphoreType.DMA((32,)),
-            pltpu.SemaphoreType.DMA((32,)),
+            pltpu.SemaphoreType.DMA((40,)),
+            pltpu.SemaphoreType.DMA((40,)),
         ],
         compiler_params=pltpu.CompilerParams(collective_id=0, has_side_effects=True),
         name="sum_everywhere",
-    )(term, weights)
+    )(term, weights, lists)
 
 
 def mid_kernel(
@@ -337,6 +354,311 @@
     )(partial, weights, time_factor, inner_inv, weight_gram)
 
 
+def invert_half(matrix):
+    down = lax.broadcasted_iota(jnp.int32, (128, 128), 0)
+    across = lax.broadcasted_iota(jnp.int32, (128, 128), 1)
+    lanes = lax.broadcasted_iota(jnp.int32, (1, 128), 1)
+    subs = lax.broadcasted_iota(jnp.int32, (128, 1), 0)
+
+    def step(t, a):
+        k0, k1 = 2 * t, 2 * t + 1
+        r0 = jnp.sum(jnp.where(down == k0, a, 0.0), axis=0, keepdims=True)
+        r1 = jnp.sum(jnp.where(down == k1, a, 0.0), axis=0, keepdims=True)
+        c0 = jnp.sum(jnp.where(across == k0, a, 0.0), axis=1, keepdims=True)
+        c1 = jnp.sum(jnp.where(across == k1, a, 0.0), axis=1, keepdims=True)
+        p00 = jnp.sum(jnp.where(lanes == k0, r0, 0.0), axis=1, keepdims=True)
+        p01 = jnp.sum(jnp.where(lanes == k1, r0, 0.0), axis=1, keepdims=True)
+        p10 = jnp.sum(jnp.where(lanes == k0, r1, 0.0), axis=1, keepdims=True)
+        p11 = jnp.sum(jnp.where(lanes == k1, r1, 0.0), axis=1, keepdims=True)
+        i0 = 1.0 / p00
+        g, h = p01 * i0, p10 * i0
+        q11 = 1.0 / (p11 - p10 * g)
+        q01, q10 = -g * q11, -h * q11
+        q00 = i0 - g * q10
+        r0 = jnp.where(lanes == k0, 1.0, jnp.where(lanes == k1, 0.0, r0))
+        r1 = jnp.where(lanes == k1, 1.0, jnp.where(lanes == k0, 0.0, r1))
+        c0 = jnp.where(subs == k0, -1.0, jnp.where(subs == k1, 0.0, c0))
+        c1 = jnp.where(subs == k1, -1.0, jnp.where(subs == k0, 0.0, c1))
+        u0, u1 = c0 * q00 + c1 * q10, c0 * q01 + c1 * q11
+        gone = (down == k0) | (down == k1) | (across == k0) | (across == k1)
+        return jnp.where(gone, 0.0, a) - u0 * r0 - u1 * r1
+
+    return lax.fori_loop(0, 64, step, matrix)
+
+
+def full_dot(a, b):
+    return jnp.dot(a, b, precision=HIGHEST, preferred_element_type=F32)
+
+
+LOW, HIGH = pl.ds(0, 128), pl.ds(128, 128)
+
+
+def invert_first(gram, out, work):
+    first = invert_half(gram[LOW, LOW])
+    out[LOW, LOW] = first
+    work[0] = full_dot(first, gram[LOW, HIGH])
+    work[1] = gram[HIGH, HIGH] - full_dot(gram[HIGH, LOW], work[0])
+
+
+def invert_second(out, work):
+    second = invert_half(work[1])
+    out[HIGH, HIGH] = second
+    cross = full_dot(work[0], second)
+    out[LOW, HIGH] = -cross
+    out[HIGH, LOW] = -cross.T
+    out[LOW, LOW] = out[LOW, LOW] + full_dot(cross, work[0].T)
+
+
+def greet_plane(y, z):
+    barrier = pltpu.get_barrier_semaphore()
+    for d in (1, 3):
+        for peer in (y_peer(y, z, d), z_peer(y, z, d)):
+            pl.semaphore_signal(
+                barrier, inc=1, device_id={"user": peer}, device_id_type=pl.DeviceIdType.MESH
+            )
+    pl.semaphore_wait(barrier, 4)
+
+
+def terms_kernel(
+    polar_all,
+    new_time,
+    weight_cols,
+    values,
+    item_gram,
+    lengths,
+    slot_of,
+    lists_y,
+    lists_z,
+    summed,
+    gram_inv,
+    terms,
+    slots,
+    got,
+    via,
+    hold,
+    out2,
+    via2,
+    fin,
+    work,
+    send_sem,
+    recv_sem,
+):
+    y, z, _, _, _ = places()
+    done = []
+
+    def go(src, dst, n, peer):
+        copy = send(src, dst, send_sem.at[n], recv_sem.at[n], user=peer)
+        copy.start()
+        done.append(copy)
+        return copy
+
+    first, second = (z, y), (y, z)
+    first_peer = (functools.partial(z_peer, y, z), functools.partial(y_peer, y, z))
+    second_peer = (functools.partial(y_peer, y, z), functools.partial(z_peer, y, z))
+    lists = (lists_z, lists_y)
+
+    def owner(h, a, b):
+        return b * 4 + a if h == 0 else a * 4 + b
+
+    greet_plane(y, z)
+    time_parts = split(new_time[...].T)
+    lanes = lax.broadcasted_iota(jnp.int32, (256, 256), 1)
+
+    def one_user(k, carry):
+        dims = (((1,), (1,)), ((), ()))
+        polar = polar_all[k]
+        maps = lax.dot_general(time_parts[0], polar, dims, preferred_element_type=F32)
+        maps = maps + lax.dot_general(time_parts[1], polar, dims, preferred_element_type=F32)
+        maps = jnp.where(lanes < lengths[k], maps * weight_cols[k], 0.0).astype(BF16)
+        for s in range(4):
+            terms[4 * k + s] = jnp.dot(
+                maps, values[4 * k + s], preferred_element_type=F32
+            ).astype(BF16)
+        return carry
+
+    lax.fori_loop(0, 16, one_user, 0)
+
+    def pack(h, d):
+        a = (first[h] + d) % 4
+
+        def one(q, carry):
+            place = owner(h, a, q // 8) * 8 + q % 8
+            slots[h, a, q] = terms[slot_of[place], pl.ds(h * 128, 128), :]
+            return carry
+
+        lax.fori_loop(0, 32, one, 0, unroll=4)
+        return a
+
+    far = {}
+    for h in range(2):
+        a = pack(h, 2)
+        far[h, 1] = go(
+            slots.at[h, a, pl.ds(0, 16)], via.at[h, 0], 12 * h, first_peer[h](1)
+        )
+        far[h, 3] = go(
+            slots.at[h, a, pl.ds(16, 16)], via.at[h, 1], 12 * h + 1, first_peer[h](3)
+        )
+    near = []
+    for h in range(2):
+        for d in (1, 3):
+            a = pack(h, d)
+            near.append(
+                go(slots.at[h, a], got.at[h, first[h]], 12 * h + 1 + d, first_peer[h](d))
+            )
+    for h in range(2):
+        pack(h, 0)
+    invert_first(item_gram, gram_inv, work)
+    for h in range(2):
+        far[h, 1].wait_recv()
+        far[h, 3].wait_recv()
+        before, after = (first[h] + 3) % 4, (first[h] + 1) % 4
+        near.append(
+            go(via.at[h, 0], got.at[h, before, pl.ds(0, 16)], 12 * h + 3, first_peer[h](1))
+        )
+        near.append(
+            go(via.at[h, 1], got.at[h, after, pl.ds(16, 16)], 12 * h + 5, first_peer[h](3))
+        )
+    invert_second(gram_inv, work)
+    arrive(near)
+
+    def dense(h, d, start, store):
+        b = (second[h] + d) % 4
+        place = owner(h, first[h], b) * 16
+
+        def one(n, carry):
+            tile = place + start + n
+            total = None
+            for e in range(4):
+                source = (first[h] + e) % 4
+                rank = lists[h][source, 1 + tile // 128, tile % 128]
+                slot = b * 8 + jnp.maximum(rank, 0)
+                block = slots[h, first[h], slot] if e == 0 else got[h, source, slot]
+                block = jnp.where(rank >= 0, block.astype(F32), 0.0)
+                total = block if total is None else total + block
+            store(n, total)
+            return carry
+
+        lax.fori_loop(0, 8, one, 0)
+
+    def into_out(h, part):
+        def store(n, total):
+            out2[h, part, n] = total.astype(BF16)
+
+        return store
+
+    def into_hold(h, part):
+        def store(n, total):
+            hold[h, part, n] = total
+
+        return store
+
+    def into_sum(h, start):
+        def store(n, total):
+            summed[start + n, pl.ds(h * 128, 128), :] = total
+
+        return store
+
+    far2 = {}
+    for h in range(2):
+        for part, start, d in ((0, 0, 1), (1, 8, 3)):
+            dense(h, 2, start, into_out(h, part))
+            far2[h, d] = go(
+                out2.at[h, part], via2.at[h, part], 12 * h + 6 + part, second_peer[h](d)
+            )
+    last = []
+    for h in range(2):
+        for part, start, d in ((2, 8, 1), (3, 0, 3)):
+            dense(h, d, start, into_out(h, part))
+            last.append(
+                go(out2.at[h, part], fin.at[h, part - 2], 12 * h + 6 + part, second_peer[h](d))
+            )
+    for h in range(2):
+        dense(h, 1, 0, into_hold(h, 0))
+        dense(h, 3, 8, into_hold(h, 1))
+    for h in range(2):
+        for part, d in ((0, 1), (1, 3)):
+            far2[h, d].wait_recv()
+
+            def merge(n, carry, h=h, part=part):
+                both = hold[h, part, n] + via2[h, part, n].astype(F32)
+                out2[h, 4 + part, n] = both.astype(BF16)
+                return carry
+
+            lax.fori_loop(0, 8, merge, 0)
+            last.append(
+                go(
+                    out2.at[h, 4 + part],
+                    fin.at[h, 2 + part],
+                    12 * h + 10 + part,
+                    second_peer[h](d),
+                )
+            )
+    for h in range(2):
+        dense(h, 0, 0, into_sum(h, 0))
+        dense(h, 0, 8, into_sum(h, 8))
+    arrive(last)
+    for h in range(2):
+        for start, parts in ((0, (1, 2)), (8, (0, 3))):
+
+            def close(n, carry, h=h, start=start, parts=parts):
+                total = summed[start + n, pl.ds(h * 128, 128), :]
+                for part in parts:
+                    total = total + fin[h, part, n].astype(F32)
+                summed[start + n, pl.ds(h * 128, 128), :] = total
+                return carry
+
+            lax.fori_loop(0, 8, close, 0)
+    for copy in done:
+        copy.wait_send()
+
+
+def sum_terms(
+    polar_all, new_time, weight_cols, values, item_gram, lengths, slot_of, lists_y, lists_z
+):
+    smem = pl.BlockSpec(memory_space=pltpu.SMEM)
+    block = (128, 128)
+    return pl.pallas_call(
+        terms_kernel,
+        out_shape=(
+            jax.ShapeDtypeStruct((16, 256, 128), F32),
+            jax.ShapeDtypeStruct((256, 256), F32),
+        ),
+        in_specs=[VMEM] * 5 + [smem] * 4,
+        out_specs=(VMEM,) * 2,
+        scratch_shapes=[
+            pltpu.VMEM((64, 256, 128), BF16),
+            pltpu.VMEM((2, 4, 32) + block, BF16),
+            pltpu.VMEM((2, 4, 32) + block, BF16),
+            pltpu.VMEM((2, 2, 16) + block, BF16),
+            pltpu.VMEM((2, 2, 8) + block, F32),
+            pltpu.VMEM((2, 6, 8) + block, BF16),
+            pltpu.VMEM((2, 2, 8) + block, BF16),
+            pltpu.VMEM((2, 4, 8) + block, BF16),
+            pltpu.VMEM((2,) + block, F32),
+            pltpu.SemaphoreType.DMA((24,)),
+            pltpu.SemaphoreType.DMA((24,)),
+        ],
+        compiler_params=pltpu.CompilerParams(collective_id=2, has_side_effects=True),
+        name="sum_terms",
+    )(polar_all, new_time, weight_cols, values, item_gram, lengths, slot_of, lists_y, lists_z)
+
+
+def tile_tables(tiles):
+    count = tiles.shape[0]
+    owners, inside = tiles // 16, tiles % 16
+    order = jnp.arange(count, dtype=jnp.int32)
+    same = (owners[:, None] == owners[None, :]) & (order[None, :] < order[:, None])
+    rank = jnp.sum(same.astype(jnp.int32), axis=1)
+    place = owners * 8 + rank
+    hit = place[None, :] == jnp.arange(128, dtype=jnp.int32)[:, None]
+    want = jnp.sum(jnp.where(hit, inside[None, :], 0), axis=1)
+    slot_of = jnp.sum(jnp.where(hit, order[None, :], 0), axis=1)
+    named = tiles[None, :] == jnp.arange(256, dtype=jnp.int32)[:, None]
+    rank_of = jnp.sum(jnp.where(named, rank[None, :] + 1, 0), axis=1) - 1
+    lists = jnp.concatenate([want, rank_of, jnp.zeros((640,), jnp.int32)]).reshape(8, 128)
+    return place, slot_of, lists
+
+
 def spd_inverse(gram):
     lower = jnp.linalg.cholesky(gram)
     return jax.scipy.linalg.cho_solve((lower, True), jnp.eye(gram.shape[0], dtype=F32))
@@ -357,7 +679,8 @@
     item_term = lax.dot_general(
         item_factor, item_factor, (((0,), (0,)), ((), ())), preferred_element_type=F32
     )
-    item_inner, all_weights = sum_everywhere(item_term, user_weights)
+    _, slot_of, lists = tile_tables(flat_ids)
+    item_inner, all_weights, lists_y, lists_z = sum_everywhere(item_term, user_weights, lists)
     all_weights = all_weights.reshape(user_count * users_here, rank_size)
     weight_gram = jnp.dot(all_weights.T, all_weights, precision=HIGHEST)
     inner_inv = spd_inverse(item_inner * weight_gram)
@@ -369,24 +692,20 @@
     polar_all, slices, new_time, item_gram = middle(
         partial, share_weights[:, None, :], time_factor, inner_inv, weight_gram
     )
-    gram_inv = spd_inverse(item_gram)
-    user_maps = (
-        jnp.einsum("krc,cd->krd", polar_all.astype(F32), new_time, precision=HIGHEST)
-        * user_weights[:, None, :]
+    values = tile_values.reshape(slot_count, time_rows, tile_width)
+    summed, gram_inv = sum_terms(
+        polar_all,
+        new_time,
+        user_weights[:, :, None],
+        values,
+        item_gram,
+        lengths,
+        slot_of,
+        lists_y,
+        lists_z,
     )
-    user_maps = jnp.where(live[:, :, None], user_maps, 0.0).astype(BF16)
-    tile_terms = jnp.einsum(
-        "ksrt,krc->kstc", tile_values, user_maps, preferred_element_type=F32
-    ).astype(BF16)
-    tile_terms = tile_terms.reshape(slot_count, tile_width * rank_size)
-    row_count = tiles_owned * tile_width * user_count
-    wanted = jnp.arange(row_count // tile_width, dtype=jnp.int32)
-    hits = (flat_ids[None, :] == wanted[:, None]).astype(BF16)
-    summed = jnp.dot(hits, tile_terms, preferred_element_type=F32)
-    item_mttkrp = lax.psum_scatter(
-        summed.reshape(row_count, rank_size).astype(BF16), "user", scatter_dimension=0, tiled=True
-    ).astype(F32)
-    new_items = jnp.dot(item_mttkrp, gram_inv, precision=HIGHEST)
+    new_items = jnp.einsum("nct,cd->ntd", summed, gram_inv, precision=HIGHEST)
+    new_items = new_items.reshape(item_factor.shape)
     return (slices, new_time, new_items)
 
 

time: 375 us -> 292 us (0.78); the launches traced: 370 us -> 291 us
  Pallas kernels: 79.2 us -> 165 us
  other arithmetic: 110 us -> 57 us
  waiting for transfers between devices: 64.7 us -> 16.3 us
  local copies, waits for them, and re-layouts: 54.1 us -> 18.7 us
  matrix products: 44.7 us -> 18.8 us
    pallas_call x0 -> x1, Pallas kernels: none -> 84.4 us  [sum_terms(): pl.pallas_call(terms_kernel, out_shape=(jax.ShapeDtypeStruct((16, 256, 12...]
    reduce_scatter x1 -> x0, waiting for transfers between devices: 45 us -> none  [body(): lax.psum_scatter(summed.reshape(row_count, rank_size).astype(BF16), 'user...]
    another operation x13 -> x6, other arithmetic: 68.8 us -> 34.1 us  [spd_inverse(): lower = jnp.linalg.cholesky(gram)]
    convert_element_type x1 -> x0, local copies, waits for them, and re-layouts: 25.6 us -> none  [body(): summed.reshape(row_count, rank_size).astype(BF16)]
    dot_general x4 -> x1, matrix products: 30 us -> 6.41 us  [body(): new_items = jnp.einsum('nct,cd->ntd', summed, gram_inv, precision=HIGHEST)]
    another operation x6 -> x4, other arithmetic: 40.3 us -> 20.4 us  [spd_inverse(): jax.scipy.linalg.cho_solve((lower, True), jnp.eye(gram.shape[0], dtype=F32))]
    another operation x15 -> x1, local copies, waits for them, and re-layouts: 7.84 us -> 0.07 us  [spd_inverse(): jax.scipy.linalg.cho_solve((lower, True), jnp.eye(gram.shape[0], dtype=F32))]
    unnamed x17 -> x12, local copies, waits for them, and re-layouts: 9.11 us -> 1.43 us
  transfers between devices with their start and end apart: 2 -> 1, of which waited for: 2 -> 1; matrix products, arithmetic and copies ran while one was open for 35% -> 25% of each run, Pallas kernels for 8% -> 11%
where the time goes in v3:
time: 292 us; the launch traced here: 291 us
  Pallas kernels  165 us (57%)
  other arithmetic  57 us (20%)
  matrix products  18.8 us (6%)
  local copies, waits for them, and re-layouts  18.7 us (6%)
  waiting for transfers between devices  16.3 us (6%)
  between operations  15.5 us (5%)
    pallas_call x1, Pallas kernels, sum_terms(): pl.pallas_call(terms_kernel, out_shape=(jax.ShapeDtypeStruct((16, 256, 12...  84.4 us
    pallas_call x1, Pallas kernels, middle(): pl.pallas_call(mid_kernel, out_shape=(jax.ShapeDtypeStruct((16, 256, 256)...  49.1 us
    another operation x6, other arithmetic, spd_inverse(): lower = jnp.linalg.cholesky(gram)  34.1 us
    pallas_call x1, Pallas kernels, sum_everywhere(): pl.pallas_call(sum_kernel, out_shape=(jax.ShapeDtypeStruct((256, 256), F3...  31.5 us
    another operation x4, other arithmetic, spd_inverse(): jax.scipy.linalg.cho_solve((lower, True), jnp.eye(gram.shape[0], dtype=F32))  20.4 us
    all_gather x1, waiting for transfers between devices, body(): shard_rows = lax.all_gather(item_factor, 'user', axis=0, tiled=True)  15.7 us
    gather x1, local copies, waits for them, and re-layouts, body(): shard_rows.reshape(tiles_owned * user_count, tile_width, rank_size)  8.51 us
    dot_general x1, matrix products, body(): new_items = jnp.einsum('nct,cd->ntd', summed, gram_inv, precision=HIGHEST)  6.41 us
  transfers between devices with their start and end apart: 1, of which 1 were waited for; matrix products, arithmetic and copies ran while one was open for 25% of the time, Pallas kernels for 11%

profile of v3, /device:TPU:1, one launch (start us, length us, event | category | flops | bytes accessed | tf_op | source)
XLA Modules:
  0.0 291.4 jit_solution(14709679270611510002)
XLA Ops:
  7.2 0.7 all-gather.2.cloned.1.call-update
  7.9 0.7 broadcast_subtract_fusion
  8.9 0.7 constant_dynamic-slice_fusion.1
  9.6 0.6 broadcast_in_dim.69.weights
  10.5 0.7 select_reduce_fusion.3
  11.2 0.6 add_bitcast_fusion.lists
  11.8 2.7 fusion.17.term
  14.5 31.5 %sum_everywhere.1 = (f32[256,256]{1,0:T(8,128)}, f32[4,4,16,256]{3,2,1,0:T(8,128)}, s32[4,8,128]{2,1,0:T(8,128)}, s32[4,8,128]{2,1,0:T(8,128)}) custom-call(f32[256,256]{1,0:T(8,128)} %fusion.17.term, f32[16,256]{1,0:T(8,128)} %weights.1, s32[8,128]{1,0:T(8,128)} %add_bitcast_fusion.lists), custom_call_target="tpu_custom_call" | custom-call | tf_op jit(solution)/shard_map/sum_everywhere/pallas_call | solution.py:171
  46.0 1.1 copy.30
  47.1 1.6 convolution_bitcast_fusion.weight_gram
  49.1 11.7 %cholesky.50 = f32[128,128]{1,0:T(8,128)S(1)} custom-call(f32[128,128]{1,0:T(8,128)S(1)} %cholesky.118), custom_call_target="Cholesky" | custom-call | tf_op jit(solution)/shard_map/jit(cholesky)/cholesky | solution.py:663
  60.9 9.8 %custom-call.18 = f32[1,128,128]{1,2,0:T(8,128)S(1)} custom-call(f32[1,128,128]{2,1,0:T(8,128)S(1)} %get-tuple-element.46), custom_call_target="InvertDiagBlocksLowerTriangular" | custom-call | tf_op jit(solution)/shard_map/jit(cholesky)/cholesky | solution.py:663
  71.2 11.9 %cholesky.105 = f32[128,128]{1,0:T(8,128)S(1)} custom-call(f32[128,128]{1,0:T(8,128)S(1)} %convolution_subtract_fusion.2), custom_call_target="Cholesky" | custom-call | tf_op jit(solution)/shard_map/jit(cholesky)/cholesky | solution.py:663
  83.1 0.6 compare_reduce_fusion
  85.1 3.8 %while.1 = (s32[]{:T(128)}, f32[256,256]{1,0:T(8,128)S(1)}, s32[2,2]{1,0:T(2,128)S(1)}, f32[2,128,128]{2,1,0:T(8,128)S(1)}, s32[]{:T(128)}) while((s32[]{:T(128)}, f32[256,256]{1,0:T(8,128)S(1)}, s32[2,2]{1,0:T(2,128)S(1)}, f32[2,128,128]{2,1,0:T(8,128)S(1)}, s32[]{:T(128)}) %tuple.30), condition=%wide.while_cond, body=%wide.while_body.sunk | while | flops 2 | bytes 131189 | solution.py:664
  85.1 0.6 fusion.33
  85.7 1.3 bitcast_dynamic-update-slice_fusion.2
  87.0 0.6 fusion.33
  87.6 1.3 bitcast_dynamic-update-slice_fusion.2
  88.9 19.7 %custom-call.19 = f32[2,128,128]{1,2,0:T(8,128)S(1)} custom-call(f32[2,128,128]{2,1,0:T(8,128)S(1)} %get-tuple-element.30), custom_call_target="InvertDiagBlocksLowerTriangular" | custom-call | tf_op jit(solution)/shard_map/jit(_cho_solve)/triangular_solve | solution.py:664
  108.6 2.0 copy.33.weight_cols
  111.2 0.3 fusion.11
  111.7 0.3 convolution_subtract_fusion
  112.3 0.7 pad_maximum_fusion.inner_inv
  113.1 15.7 %all-gather.2.cloned.1.call-done = bf16[32768,256]{1,0:T(8,128)(2,1)} async-done(((bf16[2048,256]{1,0:T(8,128)(2,1)}), bf16[32768,256]{1,0:T(8,128)(2,1)}) %all-gather.2.cloned.1.call-update) | async-done | bytes 16777232 | tf_op jit(solution)/shard_map/all_gather | solution.py:678
  128.8 8.5 %gather_fusion = bf16[64,128,256]{2,1,0:T(8,128)(2,1)} fusion(bf16[256,128,256]{2,1,0:T(8,128)(2,1)} %bitcast.69, s32[1024]{0:T(1024)S(1)} %pad_clamp_fusion), kind=kCustom, calls=%fused_computation | custom fusion | bytes 8388864 | tf_op jit(solution)/shard_map/gather | solution.py:687
  137.3 5.9 %fusion.partial = f32[16,256,256]{2,1,0:T(8,128)} fusion(bf16[16,4,256,128]{3,2,1,0:T(8,128)(2,1)} %param.6, bf16[16,4,128,256]{3,2,1,0:T(8,128)(2,1)} %bitcast.67, pred[16,256]{1,0:T(8,128)(4,1)S(1)} %iota_compare_fusion.7), kind=kOutput, calls=%fused_computation.4 | convolution fusion | flops 1074790400 | bytes 12587008 | tf_op jit(solution)/shard_map/ksrt,kstc->krc/dot_general | solution.py:689
  143.2 49.1 %middle.1 = (bf16[16,256,256]{2,1,0:T(8,128)(2,1)}, bf16[2,256,256]{2,1,0:T(8,128)(2,1)}, f32[256,256]{1,0:T(8,128)}, f32[256,256]{1,0:T(8,128)}) custom-call(f32[16,256,256]{2,1,0:T(8,128)} %fusion.partial, f32[2,1,256]{2,1,0:T(1,128)} %broadcast_in_dim.69.weights, f32[256,256]{1,0:T(8,128)} %time_factor.1, f32[256,256]{1,0:T(8,128)} %pad_maximum_fusion.inner_inv, ...), custom_call_target="tpu_custom_call" | custom-call | tf_op jit(solution)/shard_map/middle/pallas_call | solution.py:327
  192.3 84.4 %sum_terms.1 = (f32[16,256,128]{2,1,0:T(8,128)}, f32[256,256]{1,0:T(8,128)}) custom-call(bf16[16,256,256]{2,1,0:T(8,128)(2,1)} %get-tuple-element.17.polar_all, f32[256,256]{1,0:T(8,128)} %get-tuple-element.103.new_time, f32[16,256,1]{2,1,0:T(8,128)} %copy.33.weight_cols, bf16[64,256,128]{2,1,0:T(8,128)(2,1)} %bitcast.66, ...), custom_call_target="tpu_custom_call" | custom-call | tf_op jit(solution)/shard_map/sum_terms/pallas_call | solution.py:620
  276.7 6.4 %fusion.1 = f32[16,128,256]{2,1,0:T(8,128)} fusion(f32[16,256,128]{2,1,0:T(8,128)} %get-tuple-element.21, f32[256,256]{1,0:T(8,128)} %get-tuple-element.22), kind=kOutput, calls=%fused_computation.11 | convolution fusion | flops 1610612736 | bytes 4456448 | tf_op jit(solution)/shard_map/nct,cd->ntd/dot_general | solution.py:707
  283.1 0.7 copy.52
  283.8 0.7 copy.53
  (44 shorter events, 2.8 us)
Async XLA Ops:
  7.2 121.6 %all-gather.2.cloned.1.call-start = ((), (), s32[]{:S(2)}) async-start(), calls=%async_computation | async-start | bytes 17825792 | tf_op jit(solution)/shard_map/all_gather | solution.py:678
  14.5 94.1 %copy-start.3 = (f32[16,256]{1,0:T(8,128)S(1)}, f32[16,256]{1,0:T(8,128)}, u32[]{:S(2)}) copy-start(f32[16,256]{1,0:T(8,128)} %weights.1) | copy-start | bytes 49156
  48.7 63.0 %copy-start = (f32[256,256]{1,0:T(8,128)}, f32[256,256]{1,0:T(8,128)S(1)}, u32[]{:S(2)}) copy-start(f32[256,256]{1,0:T(8,128)S(1)} %convolution_bitcast_fusion.weight_gram) | copy-start | bytes 786436
  49.1 64.0 %copy-start.4 = (s32[16]{0:T(128)S(1)}, s32[16]{0:T(128)}, u32[]{:S(2)}) copy-start(s32[16]{0:T(128)} %lengths.1) | copy-start | bytes 196
  276.7 6.4 %copy-start.2 = (bf16[2,256,256]{2,1,0:T(8,128)(2,1)S(1)}, bf16[2,256,256]{2,1,0:T(8,128)(2,1)}, u32[]{:S(2)}) copy-start(bf16[2,256,256]{2,1,0:T(8,128)(2,1)} %get-tuple-element.102) | copy-start | bytes 786436
  276.7 7.1 %copy-start.1 = (f32[256,256]{1,0:T(8,128)S(1)}, f32[256,256]{1,0:T(8,128)}, u32[]{:S(2)}) copy-start(f32[256,256]{1,0:T(8,128)} %get-tuple-element.103.new_time) | copy-start | bytes 786436
Sparse Core Ops, SparseCore 0:
  10.1 118.6 all-gather.1

commit v4 on v3

--- a/solution.py
+++ b/solution.py
@@ -112,82 +112,6 @@
     for n in range(1, count):
         total = total + buf[n]
     return total
-
-
-def sum_kernel(
-    term, weights, lists, full, all_weights, lists_y, lists_z, buf_x, buf_y, buf_z, send_sem, recv_sem
-):
-    sems = (send_sem, recv_sem)
-    y, z, _, _, item = places()
-    all_weights[y, z] = weights[...]
-    lists_y[y] = lists[...]
-    lists_z[z] = lists[...]
-    greet(y, z, item)
-    started = scatter_start(term, buf_x, sems, 0, item)
-    names = []
-    for d in range(1, 4):
-        for n, held, at, peer in (
-            (32, lists_y, y, y_peer(y, z, d)),
-            (36, lists_z, z, z_peer(y, z, d)),
-        ):
-            names.append(
-                send(lists, held.at[at], send_sem.at[n + d], recv_sem.at[n + d], user=peer)
-            )
-            names[-1].start()
-    wide = []
-    for d in range(1, 4):
-        mine = all_weights.at[y, z]
-        wide.append(
-            send(mine, mine, send_sem.at[24 + d], recv_sem.at[24 + d], user=y_peer(y, z, d))
-        )
-        wide[-1].start()
-    arrive(started)
-    step = share_start(
-        buf_y, sems, 8, y, functools.partial(y_peer, y, z), total_of(buf_x, 8)
-    )
-    arrive(wide)
-    for d in range(1, 4):
-        mine = all_weights.at[:, z]
-        wide.append(
-            send(mine, mine, send_sem.at[28 + d], recv_sem.at[28 + d], user=z_peer(y, z, d))
-        )
-        wide[-1].start()
-    arrive(step)
-    started += step
-    step = share_start(
-        buf_z, sems, 12, z, functools.partial(z_peer, y, z), total_of(buf_y, 4)
-    )
-    arrive(step)
-    started += step
-    step = gather_start(full, sems, 16, item, total_of(buf_z, 4))
-    arrive(step)
-    arrive(wide[3:])
-    arrive(names)
-    for copy in started + step + wide + names:
-        copy.wait_send()
-
-
-def sum_everywhere(term, weights, lists):
-    return pl.pallas_call(
-        sum_kernel,
-        out_shape=(
-            jax.ShapeDtypeStruct((256, 256), F32),
-            jax.ShapeDtypeStruct((4, 4, 16, 256), F32),
-            jax.ShapeDtypeStruct((4, 8, 128), jnp.int32),
-            jax.ShapeDtypeStruct((4, 8, 128), jnp.int32),
-        ),
-        in_specs=[VMEM] * 3,
-        out_specs=(VMEM,) * 4,
-        scratch_shapes=[
-            pltpu.VMEM((8, 32, 256), F32),
-            pltpu.VMEM((4, 32, 256), F32),
-            pltpu.VMEM((4, 32, 256), F32),
-            pltpu.SemaphoreType.DMA((40,)),
-            pltpu.SemaphoreType.DMA((40,)),
-        ],
-        compiler_params=pltpu.CompilerParams(collective_id=0, has_side_effects=True),
-        name="sum_everywhere",
-    )(term, weights, lists)
 
 
 def mid_kernel(
@@ -643,6 +567,233 @@
     )(polar_all, new_time, weight_cols, values, item_gram, lengths, slot_of, lists_y, lists_z)
 
 
+def panels_kernel(
+    items,
+    lists,
+    weights,
+    values,
+    lengths,
+    place_of,
+    partial,
+    inner_inv,
+    weight_gram,
+    lists_y,
+    lists_z,
+    all_weights,
+    line,
+    packed,
+    got,
+    via,
+    term,
+    full,
+    buf_x,
+    buf_y,
+    buf_z,
+    work,
+    gram,
+    names_y,
+    names_z,
+    send_sem,
+    recv_sem,
+    local_sem,
+):
+    sems = (send_sem, recv_sem)
+    y, z, _, _, item = places()
+    done = []
+
+    def go(src, dst, n, peer):
+        copy = send(src, dst, send_sem.at[n], recv_sem.at[n], user=peer)
+        copy.start()
+        done.append(copy)
+        return copy
+
+    first, second = (z, y), (y, z)
+    first_peer = (functools.partial(z_peer, y, z), functools.partial(y_peer, y, z))
+    second_peer = (functools.partial(y_peer, y, z), functools.partial(z_peer, y, z))
+    wanted = (names_z, names_y)
+
+    def owner(h, a, b):
+        return b * 4 + a if h == 0 else a * 4 + b
+
+    lists_y[y] = lists[...]
+    lists_z[z] = lists[...]
+    all_weights[y, z] = weights[...]
+    greet(y, z, item)
+    names = []
+    for d in range(1, 4):
+        names.append(go(lists, lists_y.at[y], 40 + d, y_peer(y, z, d)))
+        names.append(go(lists, lists_z.at[z], 44 + d, z_peer(y, z, d)))
+    direct = {}
+    for h in range(2):
+        for d in (1, 3):
+            direct[h, d] = go(
+                items.at[:, :, pl.ds(h * 128, 128)],
+                line.at[h, second[h]],
+                48 + 4 * h + d,
+                second_peer[h](d),
+            )
+    wide = []
+    for d in range(1, 4):
+        mine = all_weights.at[y, z]
+        wide.append(go(mine, mine, 24 + d, y_peer(y, z, d)))
+    term[...] = jnp.zeros_like(term)
+
+    def add_term(n, carry):
+        tile = items[n]
+        dims = (((0,), (0,)), ((), ()))
+        term[...] += lax.dot_general(tile, tile, dims, preferred_element_type=F32)
+        return carry
+
+    lax.fori_loop(0, 16, add_term, 0)
+    step = scatter_start(term, buf_x, sems, 0, item)
+    done.extend(step)
+
+    def keep(n, carry):
+        for h in range(2):
+            line[h, second[h], n] = items[n, :, pl.ds(h * 128, 128)]
+        return carry
+
+    lax.fori_loop(0, 16, keep, 0)
+    arrive(step)
+    step = share_start(buf_y, sems, 8, y, functools.partial(y_peer, y, z), total_of(buf_x, 8))
+    done.extend(step)
+    arrive(names)
+    copies = (
+        pltpu.make_async_copy(lists_y, names_y, local_sem.at[0]),
+        pltpu.make_async_copy(lists_z, names_z, local_sem.at[1]),
+    )
+    for copy in copies:
+        copy.start()
+    arrive(wide)
+    arrive(step)
+    step = share_start(buf_z, sems, 12, z, functools.partial(z_peer, y, z), total_of(buf_y, 4))
+    done.extend(step)
+    far_wide = []
+    for d in range(1, 4):
+        mine = all_weights.at[:, z]
+        far_wide.append(go(mine, mine, 28 + d, z_peer(y, z, d)))
+    hops = []
+    for h in range(2):
+        before, after = (second[h] + 3) % 4, (second[h] + 1) % 4
+        direct[h, 1].wait_recv()
+        block = line.at[h, before, pl.ds(0, 8)]
+        hops.append(go(block, block, 48 + 4 * h, second_peer[h](1)))
+        direct[h, 3].wait_recv()
+        block = line.at[h, after, pl.ds(8, 8)]
+        hops.append(go(block, block, 50 + 4 * h, second_peer[h](3)))
+    for copy in copies:
+        copy.wait()
+    arrive(hops)
+
+    def pack(h, d):
+        a = (first[h] + d) % 4
+        out = got if d == 0 else packed
+
+        def one(q, carry):
+            b = q // 8
+            inside = wanted[h][a, 0, owner(h, first[h], b) * 8 + q % 8]
+            out[h, a, q] = line[h, b, inside]
+            return carry
+
+        lax.fori_loop(0, 32, one, 0, unroll=4)
+        return a
+
+    far = {}
+    for h in range(2):
+        a = pack(h, 2)
+        far[h, 1] = go(packed.at[h, a, pl.ds(0, 16)], via.at[h, 0], 56 + 6 * h, first_peer[h](1))
+        far[h, 3] = go(packed.at[h, a, pl.ds(16, 16)], via.at[h, 1], 57 + 6 * h, first_peer[h](3))
+    near = []
+    for h in range(2):
+        for n, d in ((58, 1), (59, 3)):
+            a = pack(h, d)
+            near.append(go(packed.at[h, a], got.at[h, first[h]], n + 6 * h, first_peer[h](d)))
+    arrive(step)
+    step = gather_start(full, sems, 16, item, total_of(buf_z, 4))
+    done.extend(step)
+    for h in range(2):
+        pack(h, 0)
+    arrive(far_wide)
+    stacked = all_weights[...].reshape(256, 256)
+    weight_gram[...] = full_dot(stacked.T, stacked)
+    arrive(step)
+    gram[...] = full[...] * weight_gram[...]
+    invert_first(gram, inner_inv, work)
+    for h in range(2):
+        before, after = (first[h] + 3) % 4, (first[h] + 1) % 4
+        far[h, 1].wait_recv()
+        near.append(
+            go(via.at[h, 0], got.at[h, before, pl.ds(0, 16)], 60 + 6 * h, first_peer[h](1))
+        )
+        far[h, 3].wait_recv()
+        near.append(
+            go(via.at[h, 1], got.at[h, after, pl.ds(16, 16)], 61 + 6 * h, first_peer[h](3))
+        )
+    invert_second(inner_inv, work)
+    arrive(near)
+    rows = lax.broadcasted_iota(jnp.int32, (256, 256), 0)
+
+    def one_user(k, carry):
+        left, right = [], []
+        for s in range(4):
+            place = place_of[4 * k + s]
+            holder, rank = place // 8, place % 8
+            at_y, at_z = holder // 4, holder % 4
+            low = got[0, at_z, at_y * 8 + rank]
+            high = got[1, at_y, at_z * 8 + rank]
+            left.append(values[4 * k + s])
+            right.append(jnp.concatenate([low, high], axis=1))
+        product = jnp.dot(
+            jnp.concatenate(left, axis=1),
+            jnp.concatenate(right, axis=0),
+            preferred_element_type=F32,
+        )
+        partial[k] = jnp.where(rows < lengths[k], product, 0.0)
+        return carry
+
+    lax.fori_loop(0, 16, one_user, 0)
+    for copy in done:
+        copy.wait_send()
+
+
+def project(items, lists, weights, values, lengths, place_of):
+    smem = pl.BlockSpec(memory_space=pltpu.SMEM)
+    block = (128, 128)
+    return pl.pallas_call(
+        panels_kernel,
+        out_shape=(
+            jax.ShapeDtypeStruct((16, 256, 256), F32),
+            jax.ShapeDtypeStruct((256, 256), F32),
+            jax.ShapeDtypeStruct((256, 256), F32),
+            jax.ShapeDtypeStruct((4, 8, 128), jnp.int32),
+            jax.ShapeDtypeStruct((4, 8, 128), jnp.int32),
+        ),
+        in_specs=[VMEM] * 4 + [smem] * 2,
+        out_specs=(VMEM,) * 5,
+        scratch_shapes=[
+            pltpu.VMEM((4, 4, 16, 256), F32),
+            pltpu.VMEM((2, 4, 16) + block, BF16),
+            pltpu.VMEM((2, 4, 32) + block, BF16),
+            pltpu.VMEM((2, 4, 32) + block, BF16),
+            pltpu.VMEM((2, 2, 16) + block, BF16),
+            pltpu.VMEM((256, 256), F32),
+            pltpu.VMEM((256, 256), F32),
+            pltpu.VMEM((8, 32, 256), F32),
+            pltpu.VMEM((4, 32, 256), F32),
+            pltpu.VMEM((4, 32, 256), F32),
+            pltpu.VMEM((2,) + block, F32),
+            pltpu.VMEM((256, 256), F32),
+            pltpu.SMEM((4, 8, 128), jnp.int32),
+            pltpu.SMEM((4, 8, 128), jnp.int32),
+            pltpu.SemaphoreType.DMA((68,)),
+            pltpu.SemaphoreType.DMA((68,)),
+            pltpu.SemaphoreType.DMA((2,)),
+        ],
+        compiler_params=pltpu.CompilerParams(collective_id=0, has_side_effects=True),
+        name="project",
+    )(items, lists, weights, values, lengths, place_of)
+
+
 def tile_tables(tiles):
     count = tiles.shape[0]
     owners, inside = tiles // 16, tiles % 16
@@ -659,11 +810,6 @@
     return place, slot_of, lists
 
 
-def spd_inverse(gram):
-    lower = jnp.linalg.cholesky(gram)
-    return jax.scipy.linalg.cho_solve((lower, True), jnp.eye(gram.shape[0], dtype=F32))
-
-
 def body(tile_values, tile_ids, lengths, user_weights, time_factor, item_factor):
     user_count = lax.axis_size("user")
     item_count = lax.axis_size("item")
@@ -674,25 +820,20 @@
     slot_count = users_here * slots_user
     share_count = users_here // item_count
     flat_ids = (tile_ids - item_pos * (tiles_owned * user_count)).reshape(slot_count)
-    live = jnp.arange(time_rows, dtype=jnp.int32)[None, :] < lengths[:, None]
-    shard_rows = lax.all_gather(item_factor, "user", axis=0, tiled=True)
-    item_term = lax.dot_general(
-        item_factor, item_factor, (((0,), (0,)), ((), ())), preferred_element_type=F32
+    place_of, slot_of, lists = tile_tables(flat_ids)
+    values = tile_values.reshape(slot_count, time_rows, tile_width)
+    partial, inner_inv, weight_gram, lists_y, lists_z = project(
+        item_factor.reshape(tiles_owned, tile_width, rank_size),
+        lists,
+        user_weights,
+        values,
+        lengths,
+        place_of,
     )
-    _, slot_of, lists = tile_tables(flat_ids)
-    item_inner, all_weights, lists_y, lists_z = sum_everywhere(item_term, user_weights, lists)
-    all_weights = all_weights.reshape(user_count * users_here, rank_size)
-    weight_gram = jnp.dot(all_weights.T, all_weights, precision=HIGHEST)
-    inner_inv = spd_inverse(item_inner * weight_gram)
-    panels = shard_rows.reshape(tiles_owned * user_count, tile_width, rank_size)[flat_ids]
-    panels = panels.reshape(users_here, slots_user, tile_width, rank_size)
-    partial = jnp.einsum("ksrt,kstc->krc", tile_values, panels, preferred_element_type=F32)
-    partial = jnp.where(live[:, :, None], partial, 0.0)
     share_weights = lax.dynamic_slice_in_dim(user_weights, item_pos * share_count, share_count, 0)
     polar_all, slices, new_time, item_gram = middle(
         partial, share_weights[:, None, :], time_factor, inner_inv, weight_gram
     )
-    values = tile_values.reshape(slot_count, time_rows, tile_width)
     summed, gram_inv = sum_terms(
         polar_all,
         new_time,

time: 292 us -> 237 us (0.81)
  Pallas kernels: 165 us -> 223 us
  other arithmetic: 57 us -> 2.19 us
  waiting for transfers between devices: 16.3 us -> 0 us
  between operations: 15.5 us -> 0.74 us
  local copies, waits for them, and re-layouts: 18.7 us -> 4.16 us
  matrix products: 18.8 us -> 6.41 us
    pallas_call x1, Pallas kernels: 31.5 us -> 90.8 us  [project(): pl.pallas_call(panels_kernel, out_shape=(jax.ShapeDtypeStruct((16, 256, 2...]
    another operation x10 -> x0, other arithmetic: 54.5 us -> none  [the longest x6 34.1 us: spd_inverse(): lower = jnp.linalg.cholesky(gram)]
    all_gather x1 -> x0, waiting for transfers between devices: 15.7 us -> none  [body(): shard_rows = lax.all_gather(item_factor, 'user', axis=0, tiled=True)]
    dot_general x3 -> x0, matrix products: 10.2 us -> none  [the longest x1 5.87 us: body(): jnp.einsum('ksrt,kstc->krc', tile_values, panels, preferred_element_type=...]
    gather x1 -> x0, local copies, waits for them, and re-layouts: 8.51 us -> none  [body(): shard_rows.reshape(tiles_owned * user_count, tile_width, rank_size)]
    another operation x9 -> x0, local copies, waits for them, and re-layouts: 3.88 us -> none
  transfers between devices with their start and end apart: 1 -> 0, of which waited for: 1 -> 0; matrix products, arithmetic and copies ran while one was open for 25% -> 0% of each run, Pallas kernels for 11% -> 0%
where the time goes in v4:
time: 237 us
  Pallas kernels  223 us (94%)
  matrix products  6.41 us (3%)
  local copies, waits for them, and re-layouts  4.16 us (2%)
    pallas_call x1, Pallas kernels, project(): pl.pallas_call(panels_kernel, out_shape=(jax.ShapeDtypeStruct((16, 256, 2...  90.8 us
    pallas_call x1, Pallas kernels, sum_terms(): pl.pallas_call(terms_kernel, out_shape=(jax.ShapeDtypeStruct((16, 256, 12...  83.8 us
    pallas_call x1, Pallas kernels, middle(): pl.pallas_call(mid_kernel, out_shape=(jax.ShapeDtypeStruct((16, 256, 256)...  48.5 us
    dot_general x1, matrix products, body(): new_items = jnp.einsum('nct,cd->ntd', summed, gram_inv, precision=HIGHEST)  6.41 us

profile of v4, /device:TPU:1, one launch (start us, length us, event | category | flops | bytes accessed | tf_op | source)
XLA Modules:
  0.0 236.6 jit_solution(18424579220129214017)
XLA Ops:
  0.6 0.7 broadcast_subtract_fusion
  1.3 0.1 copy.14
  1.4 0.1 reshape.117
  1.5 0.2 convert_reduce_fusion
  1.7 0.0 copy-start.3
  1.7 0.6 select_reduce_fusion.1
  2.3 0.1 select_reduce_fusion
  2.4 0.6 add_bitcast_fusion.lists
  3.0 0.0 copy-done.3
  3.0 0.0 copy-start.2
  3.0 90.8 %project.1 = (f32[16,256,256]{2,1,0:T(8,128)}, f32[256,256]{1,0:T(8,128)}, f32[256,256]{1,0:T(8,128)}, s32[4,8,128]{2,1,0:T(8,128)}, s32[4,8,128]{2,1,0:T(8,128)}) custom-call(bf16[16,128,256]{2,1,0:T(8,128)(2,1)} %bitcast.13, s32[8,128]{1,0:T(8,128)} %add_bitcast_fusion.lists, f32[16,256]{1,0:T(8,128)} %weights.1, bf16[64,256,128]{2,1,0:T(8,128)(2,1)} %bitcast.10, ...), custom_call_target="tpu_custom_call" | custom-call | tf_op jit(solution)/shard_map/project/pallas_call | solution.py:762
  93.8 0.0 copy-done.2
  93.9 0.6 broadcast_in_dim.54.weights
  94.4 48.5 %middle.1 = (bf16[16,256,256]{2,1,0:T(8,128)(2,1)}, bf16[2,256,256]{2,1,0:T(8,128)(2,1)}, f32[256,256]{1,0:T(8,128)}, f32[256,256]{1,0:T(8,128)}) custom-call(f32[16,256,256]{2,1,0:T(8,128)} %get-tuple-element.14.partial, f32[2,1,256]{2,1,0:T(1,128)} %broadcast_in_dim.54.weights, f32[256,256]{1,0:T(8,128)} %time_factor.1, ...), custom_call_target="tpu_custom_call" | custom-call | tf_op jit(solution)/shard_map/middle/pallas_call | solution.py:251
  143.0 2.0 copy.15.weight_cols
  144.9 83.8 %sum_terms.1 = (f32[16,256,128]{2,1,0:T(8,128)}, f32[256,256]{1,0:T(8,128)}) custom-call(bf16[16,256,256]{2,1,0:T(8,128)(2,1)} %get-tuple-element.19.polar_all, f32[256,256]{1,0:T(8,128)} %get-tuple-element.35.new_time, f32[16,256,1]{2,1,0:T(8,128)} %copy.15.weight_cols, bf16[64,256,128]{2,1,0:T(8,128)(2,1)} %bitcast.11, ...), custom_call_target="tpu_custom_call" | custom-call | tf_op jit(solution)/shard_map/sum_terms/pallas_call | solution.py:544
  228.8 0.0 copy-start.1
  228.8 0.0 copy-start
  228.8 6.4 %fusion = f32[16,128,256]{2,1,0:T(8,128)} fusion(f32[16,256,128]{2,1,0:T(8,128)} %get-tuple-element.23, f32[256,256]{1,0:T(8,128)} %get-tuple-element.24), kind=kOutput, calls=%fused_computation | convolution fusion | flops 1610612736 | bytes 4456448 | tf_op jit(solution)/shard_map/nct,cd->ntd/dot_general | solution.py:848
  235.2 0.0 copy-done.1
  235.2 0.7 copy.20
  235.9 0.0 copy-done
  235.9 0.7 copy.21
  (5 shorter events, 0.0 us)
Async XLA Ops:
  1.7 1.3 copy-start.3
  3.0 90.8 %copy-start.2 = (f32[16,256]{1,0:T(8,128)S(1)}, f32[16,256]{1,0:T(8,128)}, u32[]{:S(2)}) copy-start(f32[16,256]{1,0:T(8,128)} %weights.1) | copy-start | bytes 49156
  228.8 6.4 %copy-start.1 = (bf16[2,256,256]{2,1,0:T(8,128)(2,1)S(1)}, bf16[2,256,256]{2,1,0:T(8,128)(2,1)}, u32[]{:S(2)}) copy-start(bf16[2,256,256]{2,1,0:T(8,128)(2,1)} %get-tuple-element.34) | copy-start | bytes 786436
  228.8 7.1 %copy-start = (f32[256,256]{1,0:T(8,128)S(1)}, f32[256,256]{1,0:T(8,128)}, u32[]{:S(2)}) copy-start(f32[256,256]{1,0:T(8,128)} %get-tuple-element.35.new_time) | copy-start | bytes 786436
